TPU v7x, 256 devices: a whole 4x4x8 slice. The times are simulated.
256 devices in a mesh: dp: 4 (over x_lo, core), sp: 64 (over x_hi, z, y).
Axes of the slice: x: 4 (x_hi: 2, x_lo: 2; x = x_hi * 2 + x_lo), y: 4, z: 8, core: 2. Of those that a mesh axis runs over, the one named last changes fastest.
Arguments:
- ssm_input: bfloat16 [4, 8192, 8192], P('dp', 'sp'), may hold values from -6 to 6
- b_input: bfloat16 [4, 8192, 1024], P('dp', 'sp'), may hold values from -6 to 6
- c_input: bfloat16 [4, 8192, 1024], P('dp', 'sp'), may hold values from -6 to 6
- dt_input: bfloat16 [4, 8192, 128], P('dp', 'sp'), may hold values from -4 to 4
- conv_weight: float32 [4, 10240], replicated, may hold values from -3 to 3
- conv_bias: float32 [10240], replicated, may hold values from -3 to 3
- a_log: float32 [128], replicated, may hold values from -12 to 2
- dt_bias: float32 [128], replicated, may hold values from -5 to -3
- skip_gain: float32 [128], replicated, may hold values from 0.5 to 1.5
- grad_out: bfloat16 [4, 8192, 8192], P('dp', 'sp'), may hold values from -6 to 6
Outputs:
- y_out: bfloat16 [4, 8192, 8192], P('dp', 'sp')
- grad_x: bfloat16 [4, 8192, 8192], P('dp', 'sp')
- grad_b: bfloat16 [4, 8192, 1024], P('dp', 'sp')
- grad_c: bfloat16 [4, 8192, 1024], P('dp', 'sp')
- grad_dt: bfloat16 [4, 8192, 128], P('dp', 'sp')
- grad_conv_w: float32 [4, 10240], replicated
- grad_conv_b: float32 [10240], replicated
- grad_heads: float32 [3, 128], P(None, 'sp')
All inputs are finite; a program needn't handle non-finite values.
Results may differ from a plain program's by a relative error of at most 0.015.
Values may be sent and summed in bfloat16 or wider, within the bound.
A program may use at most 192 MiB of HBM per device.

v0:
```python
import jax
import jax.numpy as jnp
from jax import lax
from jax.sharding import PartitionSpec as P

N = 256
Q = 128


def passed_along(value, axis, by):
    devices = lax.axis_size(axis)
    pairs = [(i, i + by) for i in range(devices) if 0 <= i + by < devices]
    return lax.ppermute(value, axis, pairs)


def conv_silu(padded, kernel_cols, offset_cols):
    span = kernel_cols.shape[0]
    count_rows = padded.shape[0] - span + 1
    summed = offset_cols[None, :] + jnp.zeros((count_rows, offset_cols.shape[0]), jnp.float32)
    for tap_index in range(span):
        summed = (
            summed + kernel_cols[tap_index][None, :] * padded[tap_index : tap_index + count_rows]
        )
    return jax.nn.silu(summed)


def conv_all(x_full, b_full, c_full, kernel, offset):
    x_width = x_full.shape[1]
    b_width = b_full.shape[1]
    x_out = conv_silu(x_full, kernel[:, :x_width], offset[:x_width])
    b_out = conv_silu(
        b_full, kernel[:, x_width : x_width + b_width], offset[x_width : x_width + b_width]
    )
    c_out = conv_silu(c_full, kernel[:, x_width + b_width :], offset[x_width + b_width :])
    return (x_out, b_out, c_out)


def product(form, left, right):
    return jnp.einsum(form, left, right, preferred_element_type=jnp.float32)


def ssd_block(x_heads, dt_heads, b_group, c_group, alog_heads, dtbias_heads, skip_heads):
    length = x_heads.shape[0]
    nheads = dt_heads.shape[1]
    states = b_group.shape[1]
    hwidth = x_heads.shape[1] // nheads
    blocks = length // Q
    step_size = jax.nn.softplus(dt_heads.astype(jnp.float32) + dtbias_heads[None, :])
    steps_t = jnp.transpose(step_size).reshape(nheads, blocks, Q)
    log_t = steps_t * (-jnp.exp(alog_heads))[:, None, None]
    running = jnp.cumsum(log_t, axis=2)
    x_blocks = x_heads.reshape(blocks, Q, nheads * hwidth)
    b_blocks = b_group.reshape(blocks, Q, states)
    c_blocks = c_group.reshape(blocks, Q, states)
    scores = product("cqn,ckn->cqk", c_blocks, b_blocks)
    causal = (jnp.arange(Q)[:, None] >= jnp.arange(Q)[None, :])[None, None, :, :]
    spread_log = jnp.where(causal, running[:, :, :, None] - running[:, :, None, :], -1e30)
    mixing = (scores[None] * jnp.exp(spread_log) * steps_t[:, :, None, :]).astype(jnp.bfloat16)
    within = product("hcqk,ckhp->cqhp", mixing, x_blocks.reshape(blocks, Q, nheads, hwidth))
    to_end = jnp.exp(running[:, :, -1:] - running)
    factor = jnp.transpose(steps_t * to_end, (1, 2, 0))
    x_wide = x_blocks.astype(jnp.float32).reshape(blocks, Q, nheads, hwidth)
    weighted = (
        (x_wide * factor[:, :, :, None]).astype(jnp.bfloat16).reshape(blocks, Q, nheads * hwidth)
    )
    block_states = product("ckn,ckm->cnm", b_blocks, weighted)
    totals = running[:, :, -1]
    before = jnp.cumsum(totals, axis=1) - totals
    earlier = (jnp.arange(blocks)[:, None] > jnp.arange(blocks)[None, :])[None, :, :]
    gap_log = jnp.where(
        earlier, before[:, :, None] - before[:, None, :] - totals[:, None, :], -1e30
    )
    carried = jnp.exp(gap_log)
    entering = jnp.einsum(
        "hcd,dnhp->cnhp",
        carried,
        block_states.reshape(blocks, states, nheads, hwidth),
        precision=lax.Precision.HIGHEST,
    )
    entering_low = entering.reshape(blocks, states, nheads * hwidth).astype(jnp.bfloat16)
    across = product("cqn,cnm->cqm", c_blocks, entering_low).reshape(blocks, Q, nheads, hwidth)
    across = across * jnp.transpose(jnp.exp(running), (1, 2, 0))[:, :, :, None]
    skipped = skip_heads[None, None, :, None] * x_wide
    return (within + across + skipped).reshape(length, nheads * hwidth)


def per_device(
    ssm_input,
    b_input,
    c_input,
    dt_input,
    conv_weight,
    conv_bias,
    a_log,
    dt_bias,
    skip_gain,
    grad_out,
):
    x_rows = ssm_input[0]
    b_rows = b_input[0]
    c_rows = c_input[0]
    dt_rows = dt_input[0]
    dy_rows = grad_out[0]
    edge = conv_weight.shape[0] - 1
    devices = lax.axis_size("sp")
    my_index = lax.axis_index("sp")
    groups = b_rows.shape[1] // N
    group_devs = devices // groups
    tok_rows = x_rows.shape[0]
    rims = passed_along(
        (x_rows[tok_rows - edge :], b_rows[tok_rows - edge :], c_rows[tok_rows - edge :]), "sp", 1
    )
    x_full = jnp.concatenate([rims[0], x_rows], 0).astype(jnp.float32)
    b_full = jnp.concatenate([rims[1], b_rows], 0).astype(jnp.float32)
    c_full = jnp.concatenate([rims[2], c_rows], 0).astype(jnp.float32)
    conv_outs, conv_back = jax.vjp(conv_all, x_full, b_full, c_full, conv_weight, conv_bias)
    x_conv = conv_outs[0].astype(jnp.bfloat16)
    b_conv = conv_outs[1].astype(jnp.bfloat16)
    c_conv = conv_outs[2].astype(jnp.bfloat16)
    b_copies = jnp.broadcast_to(
        b_conv.reshape(tok_rows, groups, 1, N), (tok_rows, groups, group_devs, N)
    ).reshape(tok_rows, groups * group_devs * N)
    c_copies = jnp.broadcast_to(
        c_conv.reshape(tok_rows, groups, 1, N), (tok_rows, groups, group_devs, N)
    ).reshape(tok_rows, groups * group_devs * N)
    x_heads, dt_heads, b_group, c_group, dy_heads = (
        lax.all_to_all(x_conv, "sp", split_axis=1, concat_axis=0, tiled=True),
        lax.all_to_all(dt_rows, "sp", split_axis=1, concat_axis=0, tiled=True),
        lax.all_to_all(b_copies, "sp", split_axis=1, concat_axis=0, tiled=True),
        lax.all_to_all(c_copies, "sp", split_axis=1, concat_axis=0, tiled=True),
        lax.all_to_all(dy_rows, "sp", split_axis=1, concat_axis=0, tiled=True),
    )
    per_dev = dt_heads.shape[1]
    first_head = my_index * per_dev
    alog_heads = lax.dynamic_slice_in_dim(a_log, first_head, per_dev)
    dtbias_heads = lax.dynamic_slice_in_dim(dt_bias, first_head, per_dev)
    skip_heads = lax.dynamic_slice_in_dim(skip_gain, first_head, per_dev)
    y_heads, ssd_back = jax.vjp(
        ssd_block, x_heads, dt_heads, b_group, c_group, alog_heads, dtbias_heads, skip_heads
    )
    y_low = y_heads.astype(jnp.bfloat16)
    gx_heads, gdt_heads, gb_heads, gc_heads, galog, gdtbias, gskip = ssd_back(
        dy_heads.astype(jnp.float32)
    )
    y_rows, gx_rows, gdt_rows, gb_rows, gc_rows = (
        lax.all_to_all(y_low, "sp", split_axis=0, concat_axis=1, tiled=True),
        lax.all_to_all(gx_heads, "sp", split_axis=0, concat_axis=1, tiled=True),
        lax.all_to_all(gdt_heads, "sp", split_axis=0, concat_axis=1, tiled=True),
        lax.all_to_all(gb_heads, "sp", split_axis=0, concat_axis=1, tiled=True),
        lax.all_to_all(gc_heads, "sp", split_axis=0, concat_axis=1, tiled=True),
    )
    gb_sum = (
        gb_rows.astype(jnp.float32)
        .reshape(tok_rows, groups, group_devs, N)
        .sum(axis=2)
        .reshape(tok_rows, groups * N)
    )
    gc_sum = (
        gc_rows.astype(jnp.float32)
        .reshape(tok_rows, groups, group_devs, N)
        .sum(axis=2)
        .reshape(tok_rows, groups * N)
    )
    d_xfull, d_bfull, d_cfull, d_kernel, d_offset = conv_back(
        (gx_rows.astype(jnp.float32), gb_sum, gc_sum)
    )
    rim_back = passed_along((d_xfull[:edge], d_bfull[:edge], d_cfull[:edge]), "sp", -1)
    grad_x = d_xfull[edge:].at[tok_rows - edge :].add(rim_back[0]).astype(jnp.bfloat16)
    grad_b = d_bfull[edge:].at[tok_rows - edge :].add(rim_back[1]).astype(jnp.bfloat16)
    grad_c = d_cfull[edge:].at[tok_rows - edge :].add(rim_back[2]).astype(jnp.bfloat16)
    head_terms = jnp.stack([galog, gdtbias, gskip])
    kernel_total, offset_total = lax.psum((d_kernel, d_offset), ("dp", "sp"))
    head_total = lax.psum(head_terms, "dp")
    return (
        y_rows[None],
        grad_x[None],
        grad_b[None],
        grad_c[None],
        gdt_rows[None],
        kernel_total,
        offset_total,
        head_total,
    )


def solution(mesh):
    in_specs = (
        P("dp", "sp", None),
        P("dp", "sp", None),
        P("dp", "sp", None),
        P("dp", "sp", None),
        P(),
        P(),
        P(),
        P(),
        P(),
        P("dp", "sp", None),
    )
    out_specs = (
        P("dp", "sp", None),
        P("dp", "sp", None),
        P("dp", "sp", None),
        P("dp", "sp", None),
        P("dp", "sp", None),
        P(),
        P(),
        P(None, "sp"),
    )
    return jax.shard_map(
        per_device, mesh=mesh, in_specs=in_specs, out_specs=out_specs, check_vma=False
    )
```

profile of v0, /device:TPU:1, one launch (start us, length us, event | category | flops | bytes accessed | tf_op | source)
XLA Modules:
  0.0 1126.2 jit_solution(13000741425291463810)
XLA Ops:
  8.6 15.1 %all-to-all-start.3 = ((bf16[128,64,2]{0,2,1:T(2,128)(2,1)}), bf16[128,64,2]{0,2,1:T(2,128)(2,1)S(1)}, u32[]{:S(2)}, u32[]{:S(2)}) async-start(bf16[128,64,2]{0,2,1:T(2,128)(2,1)} %bitcast.27), calls=%async_computation.3 | async-start | bytes 65536 | tf_op jit(solution)/shard_map/all_to_all | solution.py:128
  43.5 9.1 collective-permute-done.1
  56.0 32.9 %all-to-all-done.5 = bf16[128,64,128]{0,2,1:T(8,128)(2,1)S(1)} async-done(((bf16[128,64,128]{0,2,1:T(8,128)(2,1)}), bf16[128,64,128]{0,2,1:T(8,128)(2,1)S(1)}, u32[]{:S(2)}, u32[]{:S(2)}) %all-to-all-start.5) | async-done | bytes 2097184 | tf_op jit(solution)/shard_map/all_to_all | solution.py:131
  91.4 18.2 %all-to-all-start.1 = ((bf16[128,64,256]{2,0,1:T(8,128)(2,1)}), bf16[128,64,256]{2,0,1:T(8,128)(2,1)}, u32[]{:S(2)}, u32[]{:S(2)}) async-start(bf16[128,64,256]{2,0,1:T(8,128)(2,1)} %bitcast.340), calls=%async_computation.1 | async-start | bytes 8388608 | tf_op jit(solution)/shard_map/all_to_all | solution.py:130
  112.8 14.2 %collective-permute-done.2 = bf16[3,1024]{0,1:T(8,128)(2,1)S(1)} collective-permute-done((bf16[3,1024]{0,1:T(8,128)(2,1)S(1)}, bf16[3,1024]{0,1:T(8,128)(2,1)S(1)}, u32[]{:S(2)}, u32[]{:S(2)}) %collective-permute-start.2) | collective-permute-done | bytes 6176 | tf_op jit(solution)/shard_map/ppermute | solution.py:13
  130.4 71.3 %all-to-all-done.1 = bf16[128,64,256]{2,0,1:T(8,128)(2,1)} async-done(((bf16[128,64,256]{2,0,1:T(8,128)(2,1)}), bf16[128,64,256]{2,0,1:T(8,128)(2,1)}, u32[]{:S(2)}, u32[]{:S(2)}) %all-to-all-start.1) | async-done | bytes 4194336 | tf_op jit(solution)/shard_map/all_to_all | solution.py:130
  204.1 20.1 %all-to-all-start.2 = ((bf16[128,64,256]{2,0,1:T(8,128)(2,1)}), bf16[128,64,256]{2,0,1:T(8,128)(2,1)}, u32[]{:S(2)}, u32[]{:S(2)}) async-start(bf16[128,64,256]{2,0,1:T(8,128)(2,1)} %bitcast.339), calls=%async_computation.2 | async-start | bytes 8388608 | tf_op jit(solution)/shard_map/all_to_all | solution.py:129
  245.2 71.5 %all-to-all-done.2 = bf16[128,64,256]{2,0,1:T(8,128)(2,1)} async-done(((bf16[128,64,256]{2,0,1:T(8,128)(2,1)}), bf16[128,64,256]{2,0,1:T(8,128)(2,1)}, u32[]{:S(2)}, u32[]{:S(2)}) %all-to-all-start.2) | async-done | bytes 4194336 | tf_op jit(solution)/shard_map/all_to_all | solution.py:129
  332.8 10.7 all-to-all-start.6
  353.8 38.6 %all-to-all-done.6 = bf16[64,128,128]{1,2,0:T(8,128)(2,1)} async-done(((bf16[64,128,128]{1,2,0:T(8,128)(2,1)}), bf16[64,128,128]{1,2,0:T(8,128)(2,1)}, u32[]{:S(2)}, u32[]{:S(2)}) %all-to-all-start.6) | async-done | bytes 2097184 | tf_op jit(solution)/shard_map/all_to_all | solution.py:147
  402.0 12.1 %multiply_reduce_fusion.3 = (f32[8192]{0:T(1024)S(1)}, f32[8192]{0:T(1024)}, f32[8192]{0:T(1024)}, f32[8192]{0:T(1024)}, f32[8192]{0:T(1024)}, /*index=5*/f32[128,8192]{1,0:T(8,128)}, f32[128,8192]{1,0:T(8,128)S(1)}) fusion(f32[131,8192]{1,0:T(8,128)} %maximum_convert_fusion, f32[128,8192]{1,0:T(8,128)} %copy.137, f32[8192]{0:T(1024)S(1)} %bitcast.358, ...), kind=kLoop, calls=%fused_computation.59 | loop fusion | flops 27222016 | bytes 29687808 | tf_op jit(solution)/shard_map/transpose(jvp())/reduce_sum | solution.py:22
  420.7 63.5 %all_to_all.136 = bf16[128,64,128]{0,2,1:T(8,128)(2,1)S(1)} all-to-all(bf16[128,64,128]{0,2,1:T(8,128)(2,1)} %bitcast.344), channel_id=1, replica_groups=mesh['dp'=4,'sp'=64] {'sp'}, dimensions={1} | all-to-all | bytes 4194304 | tf_op jit(solution)/shard_map/all_to_all | solution.py:127
  490.0 14.0 %fusion.110 = (f32[2,64]{1,0:T(2,128)S(1)}, f32[2,64]{1,0:T(2,128)S(1)}) fusion(f32[2,64]{1,0:T(2,128)S(1)} %slice_reduce_fusion, f32[2,64]{1,0:T(2,128)S(1)} %sub.80, f32[2,64]{1,0:T(2,128)S(1)} %subtract_reduce_fusion, f32[64,256,2,64]{1,3,2,0:T(8,128)S(1)} %bitcast.330, bf16[64,256,2,64]{1,3,2,0:T(8,128)(2,1)S(1)} %bitcast.335, ...), kind=kOutput, calls=%fused_computation.196 | convolution fusion | flops 1610669824 | bytes 12589568 | tf_op jit(solution)/shard_map/transpose(jvp(hcd,dnhp->cnhp))/dot_general | solution.py:74
  504.1 12.4 %fusion.47 = bf16[2,256,64,64]{1,3,2,0:T(8,128)(2,1)} fusion(f32[64,256,2,64]{1,3,2,0:T(8,128)S(1)} %bitcast.331, f32[2,64]{1,0:T(2,128)S(1)} %slice_reduce_fusion, f32[2,64]{1,0:T(2,128)S(1)} %sub.80, f32[2,64]{1,0:T(2,128)S(1)} %subtract_reduce_fusion, pred[64,64]{1,0:T(8,128)(4,1)S(1)} %iota_compare_fusion.1), kind=kOutput, calls=%fused_computation.70 | convolution fusion | flops 1612734464 | bytes 12588544 | tf_op jit(solution)/shard_map/jvp(hcd,dnhp->cnhp)/dot_general | solution.py:74
  517.9 11.2 fusion.12
  548.3 9.0 all-to-all-start.9
  568.1 10.8 all-to-all-start.4
  586.3 40.9 %all-to-all-done.4 = bf16[64,128,128]{1,2,0:T(8,128)(2,1)} async-done(((bf16[64,128,128]{1,2,0:T(8,128)(2,1)}), bf16[64,128,128]{1,2,0:T(8,128)(2,1)}, u32[]{:S(2)}, u32[]{:S(2)}) %all-to-all-start.4) | async-done | bytes 2097184 | tf_op jit(solution)/shard_map/all_to_all | solution.py:146
  627.1 9.2 all-to-all-start.7
  645.4 82.6 %all-to-all-done.7 = bf16[64,128,256]{2,1,0:T(8,128)(2,1)} async-done(((bf16[64,128,256]{2,1,0:T(8,128)(2,1)}), bf16[64,128,256]{2,1,0:T(8,128)(2,1)}, u32[]{:S(2)}, u32[]{:S(2)}) %all-to-all-start.7) | async-done | bytes 4194336 | tf_op jit(solution)/shard_map/all_to_all | solution.py:149
  728.0 11.3 %all-to-all-start.8 = ((bf16[64,128,256]{2,1,0:T(8,128)(2,1)}), bf16[64,128,256]{2,1,0:T(8,128)(2,1)}, u32[]{:S(2)}, u32[]{:S(2)}) async-start(bf16[64,128,256]{2,1,0:T(8,128)(2,1)} %convert_add_fusion), calls=%async_computation.8 | async-start | bytes 8388608 | tf_op jit(solution)/shard_map/all_to_all | solution.py:150
  774.8 56.6 %all-to-all-done.8 = bf16[64,128,256]{2,1,0:T(8,128)(2,1)} async-done(((bf16[64,128,256]{2,1,0:T(8,128)(2,1)}), bf16[64,128,256]{2,1,0:T(8,128)(2,1)}, u32[]{:S(2)}, u32[]{:S(2)}) %all-to-all-start.8) | async-done | bytes 4194336 | tf_op jit(solution)/shard_map/all_to_all | solution.py:150
  848.1 119.7 %psum.22 = f32[10240]{0:T(1024)} all-reduce(f32[10240]{0:T(1024)S(1)} %pad_add_fusion.6), channel_id=1, replica_groups=mesh['dp'=4,'sp'=64] {'dp','sp'}, use_global_device_ids=true, to_apply=%region_31.32 | all-reduce | flops 10240 | bytes 81920 | tf_op jit(solution)/shard_map/psum | solution.py:172
  975.4 142.3 %all-reduce.34.cloned.1.call-done = f32[4,10240]{1,0:T(4,128)} async-done(((f32[4,10240]{1,0:T(4,128)}), f32[4,10240]{1,0:T(4,128)}) %all-reduce.34.cloned.1.call-update) | async-done | bytes 163856 | tf_op jit(solution)/shard_map/psum | solution.py:172
  (219 shorter events, 213.9 us)
Async XLA Ops:
  8.6 26.0 %all-to-all-start.3 = ((bf16[128,64,2]{0,2,1:T(2,128)(2,1)}), bf16[128,64,2]{0,2,1:T(2,128)(2,1)S(1)}, u32[]{:S(2)}, u32[]{:S(2)}) async-start(bf16[128,64,2]{0,2,1:T(2,128)(2,1)} %bitcast.27), calls=%async_computation.3 | async-start | bytes 65536 | tf_op jit(solution)/shard_map/all_to_all | solution.py:128
  34.6 54.3 %all-to-all-start.5 = ((bf16[128,64,128]{0,2,1:T(8,128)(2,1)}), bf16[128,64,128]{0,2,1:T(8,128)(2,1)S(1)}, u32[]{:S(2)}, u32[]{:S(2)}) async-start(bf16[128,64,128]{0,2,1:T(8,128)(2,1)} %bitcast.343), calls=%async_computation.5 | async-start | bytes 4194304 | tf_op jit(solution)/shard_map/all_to_all | solution.py:131
  40.5 12.1 %collective-permute-start.1 = (bf16[3,1024]{0,1:T(8,128)(2,1)S(1)}, bf16[3,1024]{0,1:T(8,128)(2,1)S(1)}, u32[]{:S(2)}, u32[]{:S(2)}) collective-permute-start(bf16[3,1024]{0,1:T(8,128)(2,1)S(1)} %slice_bitcast_fusion.1), channel_id=1, source_target_pairs={{0,1},{1,2},{2,3},{3,4},{4,5},{5,6},{6,7},{7,8},{8,9},{9,10},{10,1... | collective-permute-start | bytes 18440 | tf_op jit(solution)/shard_map/ppermute | solution.py:13
  43.5 83.8 %copy-start.28 = (f32[1,1024]{1,0:T(1,128)}, f32[1,1024]{1,0:T(1,128)S(1)}, u32[]{:S(2)}) copy-start(f32[1,1024]{1,0:T(1,128)S(1)} %get-tuple-element.125) | copy-start | bytes 12292
  43.5 83.8 %copy-start.30 = (f32[1,1024]{1,0:T(1,128)}, f32[1,1024]{1,0:T(1,128)S(1)}, u32[]{:S(2)}) copy-start(f32[1,1024]{1,0:T(1,128)S(1)} %get-tuple-element.126) | copy-start | bytes 12292
  43.5 83.8 %copy-start.32 = (f32[1,1024]{1,0:T(1,128)}, f32[1,1024]{1,0:T(1,128)S(1)}, u32[]{:S(2)}) copy-start(f32[1,1024]{1,0:T(1,128)S(1)} %get-tuple-element.131) | copy-start | bytes 12292
  43.5 83.8 %copy-start.34 = (f32[1,1024]{1,0:T(1,128)}, f32[1,1024]{1,0:T(1,128)S(1)}, u32[]{:S(2)}) copy-start(f32[1,1024]{1,0:T(1,128)S(1)} %get-tuple-element.132) | copy-start | bytes 12292
  91.4 110.3 %all-to-all-start.1 = ((bf16[128,64,256]{2,0,1:T(8,128)(2,1)}), bf16[128,64,256]{2,0,1:T(8,128)(2,1)}, u32[]{:S(2)}, u32[]{:S(2)}) async-start(bf16[128,64,256]{2,0,1:T(8,128)(2,1)} %bitcast.340), calls=%async_computation.1 | async-start | bytes 8388608 | tf_op jit(solution)/shard_map/all_to_all | solution.py:130
  109.9 17.1 %collective-permute-start.2 = (bf16[3,1024]{0,1:T(8,128)(2,1)S(1)}, bf16[3,1024]{0,1:T(8,128)(2,1)S(1)}, u32[]{:S(2)}, u32[]{:S(2)}) collective-permute-start(bf16[3,1024]{0,1:T(8,128)(2,1)S(1)} %slice_bitcast_fusion), channel_id=1, source_target_pairs={{0,1},{1,2},{2,3},{3,4},{4,5},{5,6},{6,7},{7,8},{8,9},{9,10},{10,1... | collective-permute-start | bytes 18440 | tf_op jit(solution)/shard_map/ppermute | solution.py:13
  204.1 112.6 %all-to-all-start.2 = ((bf16[128,64,256]{2,0,1:T(8,128)(2,1)}), bf16[128,64,256]{2,0,1:T(8,128)(2,1)}, u32[]{:S(2)}, u32[]{:S(2)}) async-start(bf16[128,64,256]{2,0,1:T(8,128)(2,1)} %bitcast.339), calls=%async_computation.2 | async-start | bytes 8388608 | tf_op jit(solution)/shard_map/all_to_all | solution.py:129
  224.3 322.4 %copy-start.38 = (f32[2]{0:T(128)}, f32[2]{0:T(128)S(1)}, u32[]{:S(2)}) copy-start(f32[2]{0:T(128)S(1)} %dynamic_slice.9) | copy-start | bytes 28
  332.8 59.5 %all-to-all-start.6 = ((bf16[64,128,128]{1,2,0:T(8,128)(2,1)}), bf16[64,128,128]{1,2,0:T(8,128)(2,1)}, u32[]{:S(2)}, u32[]{:S(2)}) async-start(bf16[64,128,128]{1,2,0:T(8,128)(2,1)} %get-tuple-element.137), calls=%async_computation.6 | async-start | bytes 4194304 | tf_op jit(solution)/shard_map/all_to_all | solution.py:147
  344.4 5.1 collective-permute-start
  548.3 19.8 %all-to-all-start.9 = ((bf16[64,128,2]{1,2,0:T(2,128)(2,1)}), bf16[64,128,2]{1,2,0:T(2,128)(2,1)S(1)}, u32[]{:S(2)}, u32[]{:S(2)}) async-start(bf16[64,128,2]{1,2,0:T(2,128)(2,1)} %bitcast.305), calls=%async_computation.9 | async-start | bytes 65536 | tf_op jit(solution)/shard_map/all_to_all | solution.py:148
  568.1 59.0 %all-to-all-start.4 = ((bf16[64,128,128]{1,2,0:T(8,128)(2,1)}), bf16[64,128,128]{1,2,0:T(8,128)(2,1)}, u32[]{:S(2)}, u32[]{:S(2)}) async-start(bf16[64,128,128]{1,2,0:T(8,128)(2,1)} %bitcast.350), calls=%async_computation.4 | async-start | bytes 4194304 | tf_op jit(solution)/shard_map/all_to_all | solution.py:146
  586.3 50.0 %copy-start.12 = (bf16[64,128,128]{1,2,0:T(8,128)(2,1)S(1)}, bf16[64,128,128]{1,2,0:T(8,128)(2,1)}, u32[]{:S(2)}) copy-start(bf16[64,128,128]{1,2,0:T(8,128)(2,1)} %copy-done.11) | copy-start | bytes 6291460
  627.1 100.9 %all-to-all-start.7 = ((bf16[64,128,256]{2,1,0:T(8,128)(2,1)}), bf16[64,128,256]{2,1,0:T(8,128)(2,1)}, u32[]{:S(2)}, u32[]{:S(2)}) async-start(bf16[64,128,256]{2,1,0:T(8,128)(2,1)} %convert_add_fusion.1), calls=%async_computation.7 | async-start | bytes 8388608 | tf_op jit(solution)/shard_map/all_to_all | solution.py:149
  728.0 103.4 %all-to-all-start.8 = ((bf16[64,128,256]{2,1,0:T(8,128)(2,1)}), bf16[64,128,256]{2,1,0:T(8,128)(2,1)}, u32[]{:S(2)}, u32[]{:S(2)}) async-start(bf16[64,128,256]{2,1,0:T(8,128)(2,1)} %convert_add_fusion), calls=%async_computation.8 | async-start | bytes 8388608 | tf_op jit(solution)/shard_map/all_to_all | solution.py:150
  739.3 378.3 %all-reduce.34.cloned.1.call-start = ((), (), s32[]{:S(2)}) async-start(), calls=%async_computation.10 | async-start | bytes 327680 | tf_op jit(solution)/shard_map/psum | solution.py:172
  746.7 10.6 collective-permute-start.3
  774.6 61.8 %copy-start.6 = (f32[131,1024]{0,1:T(8,128)S(1)}, f32[131,1024]{0,1:T(8,128)}, u32[]{:S(2)}) copy-start(f32[131,1024]{0,1:T(8,128)} %copy-done.5) | copy-start | bytes 1609732
  774.6 61.8 %copy-start.8 = (f32[131,1024]{0,1:T(8,128)S(1)}, f32[131,1024]{0,1:T(8,128)}, u32[]{:S(2)}) copy-start(f32[131,1024]{0,1:T(8,128)} %copy-done.7) | copy-start | bytes 1609732
  845.5 122.3 %collective-permute-start.4 = (f32[3,1024]{0,1:T(8,128)S(1)}, f32[3,1024]{0,1:T(8,128)}, u32[]{:S(2)}, u32[]{:S(2)}) collective-permute-start(f32[3,1024]{0,1:T(8,128)S(1)} %slice.257), channel_id=1, source_target_pairs={{1,0},{2,1},{3,2},{4,3},{5,4},{6,5},{7,6},{8,7},{9,8},{10,9},{11,1... | collective-permute-start | bytes 36872 | tf_op jit(solution)/shard_map/ppermute | solution.py:13
  846.8 122.1 %collective-permute-start.5 = (f32[3,1024]{0,1:T(8,128)}, f32[3,1024]{0,1:T(8,128)}, u32[]{:S(2)}, u32[]{:S(2)}) collective-permute-start(f32[3,1024]{0,1:T(8,128)} %slice.260), channel_id=1, source_target_pairs={{1,0},{2,1},{3,2},{4,3},{5,4},{6,5},{7,6},{8,7},{9,8},{10,9},{11,1... | collective-permute-start | bytes 36872 | tf_op jit(solution)/shard_map/ppermute | solution.py:13
  (38 other events, 338.6 us)
Sparse Core Ops, SparseCore 0:
  845.6 271.9 all-reduce.33
where the time goes:
time: 1130 us
  waiting for transfers between devices  576 us (51%)
  blocking collectives  189 us (17%)
  starting transfers between devices  123 us (11%)
  matrix products  100 us (9%)
  other arithmetic  64.8 us (6%)
  local copies, waits for them, and re-layouts  58.1 us (5%)
  between operations  15.2 us (1%)
    psum x1, waiting for transfers between devices, per_device(): kernel_total, offset_total = lax.psum((d_kernel, d_offset), ('dp', 'sp'))  142 us
    psum x1, blocking collectives, per_device(): kernel_total, offset_total = lax.psum((d_kernel, d_offset), ('dp', 'sp'))  120 us
    all_to_all x1, waiting for transfers between devices, per_device(): lax.all_to_all(gb_heads, 'sp', split_axis=0, concat_axis=1, tiled=True)  82.6 us
    all_to_all x1, waiting for transfers between devices, per_device(): lax.all_to_all(b_copies, 'sp', split_axis=1, concat_axis=0, tiled=True)  71.5 us
    all_to_all x1, waiting for transfers between devices, per_device(): lax.all_to_all(c_copies, 'sp', split_axis=1, concat_axis=0, tiled=True)  71.3 us
    dot_general x12, matrix products, product(): return jnp.einsum(form, left, right, preferred_element_type=jnp.float32)  67.1 us
    all_to_all x1, blocking collectives, per_device(): lax.all_to_all(x_conv, 'sp', split_axis=1, concat_axis=0, tiled=True)  63.5 us
    all_to_all x1, waiting for transfers between devices, per_device(): lax.all_to_all(gc_heads, 'sp', split_axis=0, concat_axis=1, tiled=True)  56.6 us
  transfers between devices with their start and end apart: 16, of which 14 were waited for; matrix products, arithmetic and copies ran while one was open for 8% of the time, Pallas kernels for 0%

commit v1 on v0

v1 whole, which is shorter than its diff:
```python
import functools

import jax
import jax.numpy as jnp
from jax import lax
from jax.experimental import pallas as pl
from jax.experimental.pallas import tpu as pltpu
from jax.sharding import PartitionSpec as P

MESH = pl.DeviceIdType.MESH
F32 = jnp.float32
BF = jnp.bfloat16
N = 256
Q = 128
NY = 4
NB = 4
T = NB * Q
NSEG = 16
XW = 2048
CW = 256
NCH = XW // CW
HALO = 16
NPIECE = 32
HP = lax.Precision.HIGHEST
ANY = pl.BlockSpec(memory_space=pl.ANY)
VM = pl.BlockSpec(memory_space=pltpu.VMEM)
VLIM = 60 * 1024 * 1024


def dot(a, b, ca, cb):
    return lax.dot_general(a, b, (((ca,), (cb,)), ((), ())), preferred_element_type=F32)


def remote(src, dst, send, recv, target):
    return pltpu.make_async_remote_copy(
        src_ref=src, dst_ref=dst, send_sem=send, recv_sem=recv,
        device_id={"sp": target}, device_id_type=MESH,
    )


def place():
    me = lax.axis_index("sp")
    return me, lax.rem(me, NY), lax.div(me, NY)


def greet(targets, extra=None):
    barrier = pltpu.get_barrier_semaphore()
    for t in targets:
        pl.semaphore_signal(barrier, inc=1, device_id={"sp": t}, device_id_type=MESH)
    return barrier


def bring_kernel(x, dy, b, c, dt, xo, dyo, bo, co, dto, xh, bh, ch, stage, stage_s, send, recv, hs, hr, loc):
    me, y, seg = place()
    base = seg * NY
    nxt = lax.rem(seg + 1, NSEG) * NY
    prv = lax.rem(seg + NSEG - 1, NSEG) * NY + NY - 1
    peers = [base + lax.rem(y + i, NY) for i in (1, 3, 2)]
    barrier = greet(peers + [prv])

    @pl.when(y == NY - 1)
    def _():
        for j in range(NY):
            pl.semaphore_signal(barrier, inc=1, device_id={"sp": nxt + j}, device_id_type=MESH)

    pl.semaphore_wait(barrier, jnp.where(y == NY - 1, 2 * NY, NY))
    rows = pl.ds(pl.multiple_of(y * Q, Q), Q)

    def cols(j, w):
        return pl.ds(pl.multiple_of(j * w, w), w)

    arrays = ((x, xo, XW), (dy, dyo, XW), (b, bo, N), (c, co, N))

    @pl.when(y == NY - 1)
    def _():
        for j in range(NY):
            for n, (src, dst, w) in enumerate(((x, xh, XW), (b, bh, N), (c, ch, N))):
                remote(src.at[pl.ds(Q - HALO, HALO), pl.ds(j * w, w)], dst, hs.at[j, n], hr.at[n], nxt + j).start()

    copies = []
    for n, (src, dst, w) in enumerate(arrays):
        for i, k in enumerate((1, 3, 2)):
            j = lax.rem(y + k, NY)
            cp = remote(src.at[:, cols(j, w)], dst.at[rows, :], send.at[n, i], recv.at[n, i], peers[i])
            cp.start()
            copies.append(cp)
    for i in range(3):
        cp = remote(dt, dto.at[rows, :], send.at[4, i], recv.at[4, i], peers[i])
        cp.start()
        copies.append(cp)
    ins = []
    for n, (src, dst, w) in enumerate(arrays):
        st = stage.at[n] if w == XW else stage_s.at[n - 2]
        cp = pltpu.make_async_copy(src.at[:, cols(y, w)], st, loc.at[n])
        cp.start()
        ins.append((cp, st, dst))
    dst_stage = stage_s.at[2, :, pl.ds(0, 128)]
    cp = pltpu.make_async_copy(dt, dst_stage, loc.at[4])
    cp.start()
    ins.append((cp, dst_stage, dto))
    outs = []
    for n, (cp, st, dst) in enumerate(ins):
        cp.wait()
        o = pltpu.make_async_copy(st, dst.at[rows, :], loc.at[5 + n])
        o.start()
        outs.append(o)
    for o in outs:
        o.wait()
    for n, (src, dst, w) in enumerate(((x, xh, XW), (b, bh, N), (c, ch, N))):
        remote(src.at[pl.ds(Q - HALO, HALO), pl.ds(0, w)], dst, hs.at[0, n], hr.at[n], prv).wait_recv()
    for cp in copies:
        cp.wait_recv()
    for cp in copies:
        cp.wait_send()

    @pl.when(y == NY - 1)
    def _():
        for j in range(NY):
            for n, (src, dst, w) in enumerate(((x, xh, XW), (b, bh, N), (c, ch, N))):
                remote(src.at[pl.ds(Q - HALO, HALO), pl.ds(j * w, w)], dst, hs.at[j, n], hr.at[n], nxt + j).wait_send()


def bring(x, dy, b, c, dt):
    s = jax.ShapeDtypeStruct
    return pl.pallas_call(
        bring_kernel,
        name="tokens_to_heads",
        out_shape=(s((T, XW), BF), s((T, XW), BF), s((T, N), BF), s((T, N), BF), s((T, 128), BF),
                   s((HALO, XW), BF), s((HALO, N), BF), s((HALO, N), BF)),
        in_specs=[ANY] * 5,
        out_specs=[ANY] * 8,
        scratch_shapes=[
            pltpu.VMEM((2, Q, XW), BF),
            pltpu.VMEM((3, Q, N), BF),
            pltpu.SemaphoreType.DMA((5, 3)),
            pltpu.SemaphoreType.DMA((5, 3)),
            pltpu.SemaphoreType.DMA((4, 3)),
            pltpu.SemaphoreType.DMA((3,)),
            pltpu.SemaphoreType.DMA((10,)),
        ],
        compiler_params=pltpu.CompilerParams(collective_id=0, has_side_effects=True),
    )(x, dy, b, c, dt)


def spread(cols):
    lane = lax.broadcasted_iota(jnp.int32, (cols.shape[0], 128), 1) < 64
    parts = [jnp.where(lane, cols[:, h : h + 1], cols[:, h + 1 : h + 2]) for h in range(0, CW // 64, 2)]
    return jnp.concatenate(parts, axis=1)


def fill(pad, halo, raw):
    pad[0:8, :] = halo[HALO - 8 :, :].astype(F32)
    pad[8 : 8 + T, :] = raw[...].astype(F32)


def conv_rows(pad, w, bias, k):
    total = bias
    for j in range(4):
        total = total + w[j : j + 1, :] * pad[5 + j + k * Q : 5 + j + k * Q + Q, :]
    return total


def sigmoid(s):
    return 1.0 / (1.0 + jnp.exp(-s))


def local_kernel(x, xh, dy, w, bias, b, bh, c, ch, wb, wc, rs,
                 bo, co, bto, cto, so, do, pad):
    @pl.when(pl.program_id(0) == 0)
    def _():
        for raw, halo, wt, out, outt in ((b, bh, wb, bo, bto), (c, ch, wc, co, cto)):
            fill(pad, halo, raw)
            for k in range(NB):
                s = conv_rows(pad, wt[...], wt[4:5, :], k)
                v = (s * sigmoid(s)).astype(BF)
                out[k * Q : (k + 1) * Q, :] = v
                outt[:, k * Q : (k + 1) * Q] = jnp.transpose(v)

    fill(pad, xh, x)
    wx = w[...]
    S = jnp.zeros((N, CW), F32)
    for k in range(NB):
        sl = slice(k * Q, (k + 1) * Q)
        s = conv_rows(pad, wx, wx[4:5, :], k)
        xc = (s * sigmoid(s)).astype(BF).astype(F32)
        r = spread(rs[0, sl, 0:4])
        st = spread(rs[0, sl, 4:8])
        re = r[Q - 1 : Q, :]
        wt = (xc * (st * jnp.exp(re - r))).astype(BF)
        S = jnp.exp(re) * S + dot(bto[:, sl], wt, 1, 0)
    D = jnp.zeros((N, CW), F32)
    for k in reversed(range(NB)):
        sl = slice(k * Q, (k + 1) * Q)
        r = spread(rs[0, sl, 0:4])
        re = r[Q - 1 : Q, :]
        v = (dy[sl, :].astype(F32) * jnp.exp(r)).astype(BF)
        D = jnp.exp(re) * D + dot(cto[:, sl], v, 1, 0)
    for i in range(2):
        for j in range(2):
            so[2 * i + j] = S[i * 128 : (i + 1) * 128, j * 128 : (j + 1) * 128]
            do[2 * i + j] = D[i * 128 : (i + 1) * 128, j * 128 : (j + 1) * 128]


def chunked(rows):
    return pl.BlockSpec((rows, CW), lambda i: (0, i))


def whole(*shape):
    return pl.BlockSpec(shape, lambda i: (0,) * len(shape))


PIECES = pl.BlockSpec((4, 128, 128), lambda i: (i, 0, 0))
RS = pl.BlockSpec((1, T, 8), lambda i: (i, 0, 0))
RT = pl.BlockSpec((1, 8, T), lambda i: (i, 0, 0))


def local_states(x, xh, dy, w, b, bh, c, ch, wb, wc, rs):
    s = jax.ShapeDtypeStruct

    def kern(x, xh, dy, w, b, bh, c, ch, wb, wc, rs, *rest):
        local_kernel(x, xh, dy, w, None, b, bh, c, ch, wb, wc, rs, *rest)

    return pl.pallas_call(
        kern,
        name="local_states",
        grid=(NCH,),
        out_shape=(s((T, N), BF), s((T, N), BF), s((N, T), BF), s((N, T), BF),
                   s((NPIECE, 128, 128), F32), s((NPIECE, 128, 128), F32)),
        in_specs=[chunked(T), chunked(HALO), chunked(T), chunked(8), whole(T, N), whole(HALO, N),
                  whole(T, N), whole(HALO, N), whole(8, N), whole(8, N), RS],
        out_specs=[whole(T, N), whole(T, N), whole(N, T), whole(N, T), PIECES, PIECES],
        scratch_shapes=[pltpu.VMEM((T + 8, CW), F32)],
        compiler_params=pltpu.CompilerParams(vmem_limit_bytes=VLIM),
    )(x, xh, dy, w, b, bh, c, ch, wb, wc, rs)


STEP = 3


def chain_kernel(sl, dl, decay, so, do, sbuf, dbuf, ss, sr, ds, dr):
    me, y, seg = place()
    up = lax.rem(seg + 1, NSEG) * NY + y
    down = lax.rem(seg + NSEG - 1, NSEG) * NY + y
    barrier = greet([up, down])
    pl.semaphore_wait(barrier, 2)

    def half(index, first, last, loc, out, buf, send, recv, target, source):
        @pl.when((index >= 0) & (index < NPIECE))
        def _():
            @pl.when(jnp.logical_not(first))
            def _():
                remote(buf.at[index], out.at[index], send.at[index], recv.at[index], source).wait_recv()

            @pl.when(first)
            def _():
                out[index] = jnp.zeros((128, 128), BF)

            @pl.when(jnp.logical_not(last))
            def _():
                buf[index] = (out[index].astype(F32) * decay[index, 0:1, :] + loc[index]).astype(BF)
                remote(buf.at[index], out.at[index], send.at[index], recv.at[index], target).start()

    def step(n, carry):
        half(n - STEP * seg, seg == 0, seg == NSEG - 1, sl, so, sbuf, ss, sr, up, down)
        half(n - STEP * (NSEG - 1 - seg), seg == NSEG - 1, seg == 0, dl, do, dbuf, ds, dr, down, up)
        return carry

    lax.fori_loop(0, NPIECE + STEP * (NSEG - 1), step, 0)

    def drain(n, carry):
        @pl.when(seg != NSEG - 1)
        def _():
            remote(sbuf.at[n], so.at[n], ss.at[n], sr.at[n], up).wait_send()

        @pl.when(seg != 0)
        def _():
            remote(dbuf.at[n], do.at[n], ds.at[n], dr.at[n], down).wait_send()

        return carry

    lax.fori_loop(0, NPIECE, drain, 0)


def chains(sl, dl, decay):
    s = jax.ShapeDtypeStruct((NPIECE, 128, 128), BF)
    return pl.pallas_call(
        chain_kernel,
        name="state_chains",
        out_shape=(s, s),
        in_specs=[VM] * 3,
        out_specs=[VM] * 2,
        scratch_shapes=[
            pltpu.VMEM((NPIECE, 128, 128), BF),
            pltpu.VMEM((NPIECE, 128, 128), BF),
        ] + [pltpu.SemaphoreType.DMA((NPIECE,))] * 4,
        compiler_params=pltpu.CompilerParams(collective_id=1, has_side_effects=True, vmem_limit_bytes=VLIM),
    )(sl, dl, decay)


def join(ref):
    return jnp.concatenate(
        [jnp.concatenate([ref[2 * i], ref[2 * i + 1]], axis=1) for i in range(2)], axis=0
    ).astype(F32)


def conv_back(pad, dpad, w, out, last, corr, dw):
    dpad[T : T + 8, :] = jnp.zeros((8, pad.shape[1]), F32)
    sums = [jnp.zeros((1, pad.shape[1]), F32) for _ in range(5)]
    for k in range(NB):
        d0 = dpad[k * Q : (k + 1) * Q, :]
        for j in range(4):
            sums[j] = sums[j] + jnp.sum(d0 * pad[5 + j + k * Q : 5 + j + k * Q + Q, :], axis=0, keepdims=True)
        sums[4] = sums[4] + jnp.sum(d0, axis=0, keepdims=True)
        g = w[3:4, :] * d0
        for j in range(3):
            g = g + w[j : j + 1, :] * dpad[3 - j + k * Q : 3 - j + (k + 1) * Q, :]
        out[k * Q : (k + 1) * Q, :] = g.astype(BF)
        if k == NB - 1:
            last[...] = g[Q - 16 :, :]
    z = jnp.zeros((1, pad.shape[1]), F32)
    d = [dpad[m : m + 1, :] for m in range(3)]
    ws = [w[j : j + 1, :] for j in range(3)]
    corr[...] = jnp.concatenate(
        [z] * 5 + [ws[0] * d[0], ws[1] * d[0] + ws[0] * d[1], ws[2] * d[0] + ws[1] * d[1] + ws[0] * d[2]], axis=0
    )
    dw[...] = jnp.concatenate(sums + [z] * 3, axis=0)


def final_kernel(x, xh, dy, w, b, bh, c, ch, wb, wc, rs, rt, skip, bc, cc, bct, cct, sin, din,
                 yo, gxo, xlast, xcorr, xdw, gbo, blast, bcorr, bdw, gco, clast, ccorr, cdw, qo, dso,
                 pad, dpad, S, sc, gacc, db, dc):
    pid = pl.program_id(0)

    @pl.when(pid == 0)
    def _():
        for k in range(NB):
            sl = slice(k * Q, (k + 1) * Q)
            sc[k] = dot(cc[sl, :], bc[sl, :], 1, 1)
        gacc[...] = jnp.zeros_like(gacc)
        db[...] = jnp.zeros_like(db)
        dc[...] = jnp.zeros_like(dc)
        qo[...] = jnp.zeros_like(qo)

    fill(pad, xh, x)
    wx = w[...]
    S[0] = join(sin)
    for k in range(NB):
        sl = slice(k * Q, (k + 1) * Q)
        s = conv_rows(pad, wx, wx[4:5, :], k)
        xc = (s * sigmoid(s)).astype(BF).astype(F32)
        r = spread(rs[0, sl, 0:4])
        st = spread(rs[0, sl, 4:8])
        re = r[Q - 1 : Q, :]
        wt = (xc * (st * jnp.exp(re - r))).astype(BF)
        S[k + 1] = jnp.exp(re) * S[k] + dot(bct[:, sl], wt, 1, 0)

    D = join(din)
    causal = lax.broadcasted_iota(jnp.int32, (Q, Q), 0) >= lax.broadcasted_iota(jnp.int32, (Q, Q), 1)
    low = lax.broadcasted_iota(jnp.int32, (Q, 128), 1) < 64
    er = lax.broadcasted_iota(jnp.int32, (CW, 128), 0) // 64 + pid * (CW // 64)
    el = lax.broadcasted_iota(jnp.int32, (CW, 128), 1)
    ends = []
    for k in reversed(range(NB)):
        sl = slice(k * Q, (k + 1) * Q)
        s = conv_rows(pad, wx, wx[4:5, :], k)
        sg = sigmoid(s)
        xcb = (s * sg).astype(BF)
        xc = xcb.astype(F32)
        dyb = dy[sl, :]
        dyf = dyb.astype(F32)
        rc = rs[0, sl, 0:4]
        r = spread(rc)
        st = spread(rs[0, sl, 4:8])
        re = r[Q - 1 : Q, :]
        er_ = jnp.exp(r)
        ee = jnp.exp(re - r)
        ub = (xc * st).astype(BF)
        wt = (xc * (st * ee)).astype(BF)
        v = (dyf * er_).astype(BF)
        Sb = S[k].astype(BF)
        Db = D.astype(BF)
        ends.append(jnp.sum(D * S[k + 1], axis=0, keepdims=True))
        ya = er_ * dot(cc[sl, :], Sb, 1, 0)
        du = ee * dot(bc[sl, :], Db, 1, 0)
        db[sl, :] += dot(wt, Db, 1, 1)
        dc[sl, :] += dot(v, Sb, 1, 1)
        yw, dw_ = [], []
        g = sc[k]
        acc = gacc[k]
        zero = jnp.zeros((Q, 128), BF)
        for p in range(CW // 128):
            ls = []
            for h in (2 * p, 2 * p + 1):
                gap = rc[:, h : h + 1] - rt[0, h : h + 1, sl]
                ls.append(jnp.exp(jnp.where(causal, gap, -1e30)))
            up = ub[:, p * 128 : (p + 1) * 128]
            dp = dyb[:, p * 128 : (p + 1) * 128]
            ublk = jnp.concatenate([jnp.where(low, up, zero), jnp.where(low, zero, up)], axis=0)
            dblk = jnp.concatenate([jnp.where(low, dp, zero), jnp.where(low, zero, dp)], axis=0)
            ms = [(g * l).astype(BF) for l in ls]
            yw.append(dot(jnp.concatenate(ms, axis=1), ublk, 1, 0))
            dw_.append(dot(jnp.concatenate(ms, axis=0), dblk, 0, 0))
            dm = dot(dp, ublk, 1, 1)
            acc = acc + dm[:, :Q] * ls[0] + dm[:, Q:] * ls[1]
        gacc[k] = acc
        yin = ya + jnp.concatenate(yw, axis=1)
        du = du + jnp.concatenate(dw_, axis=1)
        sk = skip[0:1, :]
        yo[sl, :] = (yin + sk * xc).astype(BF)
        qs = (dyf * yin - ub.astype(F32) * du, xc * du, dyf * xc)
        total = jnp.zeros((Q, 128), F32)
        for i, q in enumerate(qs):
            e = (el == er + 32 * i).astype(BF)
            hi = q.astype(BF)
            lo = (q - hi.astype(F32)).astype(BF)
            total = total + dot(hi, e, 1, 0) + dot(lo, e, 1, 0)
        qo[sl, :] += total
        gx = st * du + sk * dyf
        dpad[sl, :] = gx * (sg * (1.0 + s * (1.0 - sg)))
        D = jnp.exp(re) * D + dot(cct[:, sl], v, 1, 0)
    dso[...] = jnp.concatenate(ends[::-1] + [jnp.zeros((4, CW), F32)], axis=0)
    conv_back(pad, dpad, wx, gxo, xlast, xcorr, xdw)

    @pl.when(pid == NCH - 1)
    def _():
        for raw, halo, wt, gout, lst, crr, dwo, acc, other, tr in (
            (b, bh, wb, gbo, blast, bcorr, bdw, db, cc, True),
            (c, ch, wc, gco, clast, ccorr, cdw, dc, bc, False),
        ):
            fill(pad, halo, raw)
            for k in range(NB):
                sl = slice(k * Q, (k + 1) * Q)
                gk = gacc[k].astype(BF)
                tot = acc[sl, :] + dot(gk, other[sl, :], 0 if tr else 1, 0)
                s = conv_rows(pad, wt[...], wt[4:5, :], k)
                sg = sigmoid(s)
                dpad[sl, :] = tot * (sg * (1.0 + s * (1.0 - sg)))
            conv_back(pad, dpad, wt[...], gout, lst, crr, dwo)


def finals(x, xh, dy, w, b, bh, c, ch, wb, wc, rs, rt, skip, bc, cc, bct, cct, sin, din):
    s = jax.ShapeDtypeStruct
    bx = [whole(T, N), whole(16, N), whole(8, N), whole(8, N)]
    bs = [s((T, N), BF), s((16, N), F32), s((8, N), F32), s((8, N), F32)]
    return pl.pallas_call(
        final_kernel,
        name="outputs_and_gradients",
        grid=(NCH,),
        out_shape=[s((T, XW), BF), s((T, XW), BF), s((16, XW), F32), s((8, XW), F32), s((8, XW), F32)]
        + bs + bs + [s((T, 128), F32), s((8, XW), F32)],
        in_specs=[chunked(T), chunked(HALO), chunked(T), chunked(8), whole(T, N), whole(HALO, N),
                  whole(T, N), whole(HALO, N), whole(8, N), whole(8, N), RS, RT, chunked(8),
                  whole(T, N), whole(T, N), whole(N, T), whole(N, T), PIECES, PIECES],
        out_specs=[chunked(T), chunked(T), chunked(16), chunked(8), chunked(8)] + bx + bx
        + [whole(T, 128), chunked(8)],
        scratch_shapes=[
            pltpu.VMEM((T + 8, CW), F32),
            pltpu.VMEM((T + 8, CW), F32),
            pltpu.VMEM((NB + 1, N, CW), F32),
            pltpu.VMEM((NB, Q, Q), F32),
            pltpu.VMEM((NB, Q, Q), F32),
            pltpu.VMEM((T, N), F32),
            pltpu.VMEM((T, N), F32),
        ],
        compiler_params=pltpu.CompilerParams(vmem_limit_bytes=VLIM),
    )(x, xh, dy, w, b, bh, c, ch, wb, wc, rs, rt, skip, bc, cc, bct, cct, sin, din)


def give_kernel(yf, gx, gb, gc, gdt, lx, lb, lc, kx, kb, kc,
                yo, gxo, gbo, gco, gdo,
                stage, stage_s, hx, hb, hc, tx, tb, tc, dts, send, recv, ks, kr, ts, tr, loc):
    me, y, seg = place()
    base = seg * NY
    up = lax.rem(seg + 1, NSEG) * NY + y
    down = lax.rem(seg + NSEG - 1, NSEG) * NY + y
    peers = [base + lax.rem(y + i, NY) for i in (1, 3, 2)]
    barrier = greet(peers + [up, down])
    pl.semaphore_wait(barrier, 5)
    halos = [remote(src, dst, ks.at[n], kr.at[n], down) for n, (src, dst) in enumerate(((kx, hx), (kb, hb), (kc, hc)))]
    for cp in halos:
        cp.start()

    def cols(w):
        return pl.ds(pl.multiple_of(y * w, w), w)

    arrays = ((yf, yo, XW, Q), (gx, gxo, XW, Q - 16), (gb, gbo, N, Q - 16), (gc, gco, N, Q - 16))
    copies = []
    for n, (src, dst, w, rows) in enumerate(arrays):
        for i, k in enumerate((1, 3, 2)):
            j = lax.rem(y + k, NY)
            rs = pl.ds(pl.multiple_of(j * Q, Q), rows)
            cp = remote(src.at[rs, :], dst.at[pl.ds(0, rows), cols(w)], send.at[n, i], recv.at[n, i], peers[i])
            cp.start()
            copies.append(cp)
    for i, k in enumerate((1, 3, 2)):
        j = lax.rem(y + k, NY)
        rs = pl.ds(pl.multiple_of(j * Q, Q), Q)
        cp = remote(gdt.at[rs, :], dts.at[i], send.at[4, i], recv.at[4, i], peers[i])
        cp.start()
        copies.append(cp)
    mine = pl.ds(pl.multiple_of(y * Q, Q), Q)
    tails = ((gx, gxo, XW, tx), (gb, gbo, N, tb), (gc, gco, N, tc))
    for n, (cp, t, l, h) in enumerate(zip(halos, (tx, tb, tc), (lx, lb, lc), (hx, hb, hc))):
        cp.wait_recv()

        @pl.when(seg == NSEG - 1)
        def _():
            t[...] = l[...].astype(BF)

        @pl.when(seg != NSEG - 1)
        def _():
            t[0:8, :] = l[0:8, :].astype(BF)
            t[8:16, :] = (l[8:16, :] + h[...]).astype(BF)

    def tail(n, i, k, do):
        src, dst, w, t = tails[n]
        j = lax.rem(y + k, NY)
        place_to = dst.at[pl.ds(Q - 16, 16), cols(w)]

        @pl.when(j == NY - 1)
        def _():
            do(remote(t, place_to, ts.at[n, i], tr.at[n, i], peers[i]))

        @pl.when(j != NY - 1)
        def _():
            rs = pl.ds(pl.multiple_of(j * Q + Q - 16, 16), 16)
            do(remote(src.at[rs, :], place_to, ts.at[n, i], tr.at[n, i], peers[i]))

    for n in range(3):
        for i, k in enumerate((1, 3, 2)):
            tail(n, i, k, lambda cp: cp.start())
    ins = []
    for n, (src, dst, w, rows) in enumerate(arrays):
        st = stage.at[n] if w == XW else stage_s.at[n - 2]
        cp = pltpu.make_async_copy(src.at[mine, :], st, loc.at[n])
        cp.start()
        ins.append((cp, st, dst, w))
    outs = []
    for n, (cp, st, dst, w) in enumerate(ins):
        cp.wait()
        if n > 0:
            t = tails[n - 1][3]

            @pl.when(y == NY - 1)
            def _():
                st[Q - 16 :, :] = t[...]

        o = pltpu.make_async_copy(st, dst.at[:, cols(w)], loc.at[4 + n])
        o.start()
        outs.append(o)
    own = pltpu.make_async_copy(gdt.at[mine, :], dts.at[3], loc.at[8])
    own.start()
    own.wait()
    for cp in copies[12:]:
        cp.wait_recv()
    gdo[...] = (dts[0].astype(F32) + dts[1].astype(F32) + dts[2].astype(F32) + dts[3].astype(F32)).astype(BF)
    for o in outs:
        o.wait()
    for cp in copies[:12]:
        cp.wait_recv()
    for n in range(3):
        for i, k in enumerate((1, 3, 2)):
            tail(n, i, k, lambda cp: cp.wait())
    for cp in copies:
        cp.wait_send()
    for cp in halos:
        cp.wait_send()


def give(*args):
    s = jax.ShapeDtypeStruct
    return pl.pallas_call(
        give_kernel,
        name="heads_to_tokens",
        out_shape=(s((Q, NY * XW), BF), s((Q, NY * XW), BF), s((Q, NY * N), BF), s((Q, NY * N), BF), s((Q, 128), BF)),
        in_specs=[ANY] * 5 + [VM] * 6,
        out_specs=[ANY] * 4 + [VM],
        scratch_shapes=[
            pltpu.VMEM((2, Q, XW), BF),
            pltpu.VMEM((2, Q, N), BF),
            pltpu.VMEM((8, XW), F32), pltpu.VMEM((8, N), F32), pltpu.VMEM((8, N), F32),
            pltpu.VMEM((16, XW), BF), pltpu.VMEM((16, N), BF), pltpu.VMEM((16, N), BF),
            pltpu.VMEM((4, Q, 128), BF),
            pltpu.SemaphoreType.DMA((5, 3)),
            pltpu.SemaphoreType.DMA((5, 3)),
            pltpu.SemaphoreType.DMA((3,)),
            pltpu.SemaphoreType.DMA((3,)),
            pltpu.SemaphoreType.DMA((3, 3)),
            pltpu.SemaphoreType.DMA((3, 3)),
            pltpu.SemaphoreType.DMA((9,)),
        ],
        compiler_params=pltpu.CompilerParams(collective_id=2, has_side_effects=True),
    )(*args)


def total_kernel(v, out, ra, rb, part, mid, s1, r1, s2, r2, s3, r3):
    dp = lax.axis_index("dp")
    me, y, seg = place()
    xh = lax.div(seg, 8)
    z = lax.rem(seg, 8)

    def to(d, h, zz, yy):
        return {"dp": d, "sp": h * 32 + zz * 4 + yy}

    along_z = [to(dp, xh, lax.rem(z + i, 8), y) for i in range(1, 8)]
    pos = dp * 2 + xh
    along_x = []
    for i in range(1, 8):
        q = lax.rem(pos + i, 8)
        along_x.append(to(lax.div(q, 2), lax.rem(q, 2), z, y))
    pzy = z * 4 + y
    along_zy = []
    for i in range(1, 32):
        q = lax.rem(pzy + i, 32)
        along_zy.append({"dp": dp, "sp": xh * 32 + q})
    barrier = pltpu.get_barrier_semaphore()
    for t in along_x + along_zy:
        pl.semaphore_signal(barrier, inc=1, device_id=t, device_id_type=MESH)
    pl.semaphore_wait(barrier, 38)

    def send(src, dst, a, b, t):
        cp = pltpu.make_async_remote_copy(src_ref=src, dst_ref=dst, send_sem=a, recv_sem=b, device_id=t, device_id_type=MESH)
        cp.start()
        return cp

    def block(i):
        return pl.ds(pl.multiple_of(i * 16, 16), 16)

    first = [send(v.at[block(lax.rem(z + i + 1, 8)), :], ra.at[z], s1.at[i], r1.at[i], t) for i, t in enumerate(along_z)]
    ra[z] = v[block(z), :]
    for cp in first:
        cp.wait()
    tot = ra[0]
    for i in range(1, 8):
        tot = tot + ra[i]
    part[...] = tot
    rb[pos] = tot
    second = [send(part, rb.at[pos], s2.at[i], r2.at[i], t) for i, t in enumerate(along_x)]
    for cp in second:
        cp.wait()
    tot = rb[0]
    for i in range(1, 8):
        tot = tot + rb[i]
    mid[...] = tot
    out[y, block(z), :] = tot
    third = [send(mid, out.at[y, block(z), :], s3.at[i], r3.at[i], t) for i, t in enumerate(along_zy)]
    for cp in third:
        cp.wait()


def totals(v):
    return pl.pallas_call(
        total_kernel,
        name="small_sums",
        out_shape=jax.ShapeDtypeStruct((NY, 128, 128), F32),
        in_specs=[VM],
        out_specs=VM,
        scratch_shapes=[
            pltpu.VMEM((8, 16, 128), F32),
            pltpu.VMEM((8, 16, 128), F32),
            pltpu.VMEM((16, 128), F32),
            pltpu.VMEM((16, 128), F32),
            pltpu.SemaphoreType.DMA((7,)), pltpu.SemaphoreType.DMA((7,)),
            pltpu.SemaphoreType.DMA((7,)), pltpu.SemaphoreType.DMA((7,)),
            pltpu.SemaphoreType.DMA((31,)), pltpu.SemaphoreType.DMA((31,)),
        ],
        compiler_params=pltpu.CompilerParams(collective_id=3, has_side_effects=True),
    )(v)


def per_device(ssm_input, b_input, c_input, dt_input, conv_weight, conv_bias, a_log, dt_bias, skip_gain, grad_out):
    me = lax.axis_index("sp")
    y = lax.rem(me, NY)
    seg = lax.div(me, NY)
    x, dy, b, c, dt, xh, bh, ch = bring(ssm_input[0], grad_out[0], b_input[0], c_input[0], dt_input[0])
    first = seg == 0
    xh, bh, ch = [jnp.where(first, jnp.zeros_like(h), h) for h in (xh, bh, ch)]
    taps = jnp.concatenate([conv_weight, conv_bias[None], jnp.zeros((3, conv_weight.shape[1]), F32)], 0)
    w = lax.dynamic_slice_in_dim(taps, y * XW, XW, 1)
    wb = lax.dynamic_slice_in_dim(taps, NY * XW + y * N, N, 1)
    wc = lax.dynamic_slice_in_dim(taps, NY * (XW + N) + y * N, N, 1)
    heads = XW // 64

    def own(v):
        return lax.dynamic_slice_in_dim(v, y * heads, heads, 0)

    rate = jnp.exp(own(a_log))
    raw = lax.dynamic_slice_in_dim(dt, y * heads, heads, 1).astype(F32) + own(dt_bias)[None, :]
    step = jax.nn.softplus(raw)
    logs = -step * rate[None, :]
    tril = (jnp.arange(Q)[:, None] >= jnp.arange(Q)[None, :]).astype(F32)
    run = jnp.einsum("ts,ksh->kth", tril, logs.reshape(NB, Q, heads), precision=HP)
    whole_decay = jnp.exp(run[:, -1, :].sum(0))
    run = run.reshape(T, heads)
    per = CW // 64
    rs = jnp.concatenate([run.reshape(T, NCH, per), step.reshape(T, NCH, per)], 2).transpose(1, 0, 2)
    rt = jnp.pad(run.reshape(T, NCH, per).transpose(1, 2, 0), ((0, 0), (0, 8 - per), (0, 0)))
    skip = jnp.broadcast_to(jnp.repeat(own(skip_gain), 64)[None, :], (8, XW))
    lanes = jnp.repeat(whole_decay, 64).reshape(NCH, 1, 2, 128)
    decay = jnp.broadcast_to(lanes, (NCH, 2, 2, 128)).reshape(NPIECE, 1, 128)
    decay = jnp.broadcast_to(decay, (NPIECE, 8, 128))
    bc, cc, bct, cct, sl, dl = local_states(x, xh, dy, w, b, bh, c, ch, wb, wc, rs)
    sin, din = chains(sl, dl, decay)
    (yf, gx, xlast, xcorr, xdw, gb, blast, bcorr, bdw, gc, clast, ccorr, cdw, qs, ends) = finals(
        x, xh, dy, w, b, bh, c, ch, wb, wc, rs, rt, skip, bc, cc, bct, cct, sin, din
    )
    q1 = qs[:, :heads].reshape(NB, Q, heads)
    end = ends[:NB].reshape(NB, heads, 64).sum(-1)
    dlog = (jnp.einsum("ts,kth->ksh", tril, q1, precision=HP) + end[:, None, :]).reshape(T, heads)
    dstep = qs[:, heads : 2 * heads] - dlog * rate[None, :]
    draw = dstep * jax.nn.sigmoid(raw)
    gdt = jnp.zeros((T, 128), BF)
    gdt = lax.dynamic_update_slice_in_dim(gdt, draw.astype(BF), y * heads, 1)
    hg = jnp.stack([(dlog * logs).sum(0), draw.sum(0), qs[:, 2 * heads : 3 * heads].sum(0)])
    v = jnp.concatenate([xdw[:5], bdw[:5], cdw[:5]], 1).reshape(100, 128)
    hrow = jnp.pad(hg.reshape(1, 3 * heads), ((0, 27), (0, 128 - 3 * heads)))
    tot = totals(jnp.concatenate([v, hrow], 0))
    grads = tot[:, :100, :].reshape(NY, 5, XW + 2 * N).transpose(1, 0, 2)
    gw = jnp.concatenate(
        [grads[:, :, :XW].reshape(5, -1), grads[:, :, XW : XW + N].reshape(5, -1), grads[:, :, XW + N :].reshape(5, -1)], 1
    )
    hsum = tot[:, 100, : 3 * heads].reshape(NY, 3, heads).transpose(1, 0, 2).reshape(3, NY * heads)
    hsum = lax.dynamic_slice_in_dim(hsum, me * 2, 2, 1)
    yo, gxo, gbo, gco, gdo = give(yf, gx, gb, gc, gdt, xlast, blast, clast, xcorr, bcorr, ccorr)
    return (yo[None], gxo[None], gbo[None], gco[None], gdo[None], gw[:4], gw[4], hsum)


def solution(mesh):
    row = P("dp", "sp", None)
    return jax.shard_map(
        per_device, mesh=mesh,
        in_specs=(row, row, row, row, P(), P(), P(), P(), P(), row),
        out_specs=(row, row, row, row, row, P(), P(), P(None, "sp")),
        check_vma=False,
    )
```

time: 1130 us -> 339 us (0.30)
  waiting for transfers between devices: 576 us -> 0 us
  Pallas kernels: 0 us -> 310 us
  blocking collectives: 189 us -> 0 us
  starting transfers between devices: 123 us -> 0 us
  matrix products: 100 us -> 1.68 us
  other arithmetic: 64.8 us -> 6.51 us
  local copies, waits for them, and re-layouts: 58.1 us -> 19.6 us
  between operations: 15.2 us -> 0.92 us
    all_to_all x9 -> x0, waiting for transfers between devices: 403 us -> none  [the longest x1 82.6 us: per_device(): lax.all_to_all(gb_heads, 'sp', split_axis=0, concat_axis=1, tiled=True)]
    pallas_call x0 -> x6, Pallas kernels: none -> 310 us  [the longest x1 77.2 us: chains(): pl.pallas_call(chain_kernel, name='state_chains', out_shape=(s, s), in_sp...]
    psum x1 -> x0, waiting for transfers between devices: 142 us -> none  [per_device(): kernel_total, offset_total = lax.psum((d_kernel, d_offset), ('dp', 'sp'))]
    psum x2 -> x0, blocking collectives: 125 us -> none  [the longest x1 120 us: per_device(): kernel_total, offset_total = lax.psum((d_kernel, d_offset), ('dp', 'sp'))]
    all_to_all x9 -> x0, starting transfers between devices: 110 us -> none  [the longest x1 20.1 us: per_device(): lax.all_to_all(b_copies, 'sp', split_axis=1, concat_axis=0, tiled=True)]
    dot_general x15 -> x2, matrix products: 100 us -> 1.68 us  [the longest x1 1.32 us: per_device(): jnp.einsum('ts,kth->ksh', tril, q1, precision=HP) + end[:, None, :]]
    all_to_all x1 -> x0, blocking collectives: 63.5 us -> none  [per_device(): lax.all_to_all(x_conv, 'sp', split_axis=1, concat_axis=0, tiled=True)]
    ppermute x6 -> x0, waiting for transfers between devices: 30.5 us -> none  [passed_along(): return lax.ppermute(value, axis, pairs)]
  transfers between devices with their start and end apart: 16 -> 0, of which waited for: 14 -> 0; matrix products, arithmetic and copies ran while one was open for 8% -> 0% of each run, Pallas kernels for 0% -> 0%
where the time goes in v1:
time: 339 us
  Pallas kernels  310 us (91%)
  local copies, waits for them, and re-layouts  19.6 us (6%)
  other arithmetic  6.51 us (2%)
    pallas_call x1, Pallas kernels, chains(): pl.pallas_call(chain_kernel, name='state_chains', out_shape=(s, s), in_sp...  77.2 us
    pallas_call x1, Pallas kernels, bring(): pl.pallas_call(bring_kernel, name='tokens_to_heads', out_shape=(s((T, XW)...  66.7 us
    pallas_call x1, Pallas kernels, give(): pl.pallas_call(give_kernel, name='heads_to_tokens', out_shape=(s((Q, NY *...  61.8 us
    pallas_call x1, Pallas kernels, finals(): pl.pallas_call(final_kernel, name='outputs_and_gradients', grid=(NCH,), o...  46.2 us
    pallas_call x1, Pallas kernels, totals(): pl.pallas_call(total_kernel, name='small_sums', out_shape=jax.ShapeDtypeS...  43.5 us
    pallas_call x1, Pallas kernels, local_states(): pl.pallas_call(kern, name='local_states', grid=(NCH,), out_shape=(s((T, N...  14.4 us
    unnamed x30, local copies, waits for them, and re-layouts  7.94 us

profile of v1, /device:TPU:1, one launch (start us, length us, event | category | flops | bytes accessed | tf_op | source)
XLA Modules:
  0.0 338.5 jit_solution(7000729064188492371)
XLA Ops:
  0.6 0.7 dynamic-slice_exponential_fusion
  1.4 0.7 dynamic_slice.28
  2.1 66.7 %tokens_to_heads.1 = (bf16[512,2048]{1,0:T(8,128)(2,1)}, bf16[512,2048]{1,0:T(8,128)(2,1)}, bf16[512,256]{1,0:T(8,128)(2,1)}, bf16[512,256]{1,0:T(8,128)(2,1)}, ...) custom-call(bf16[128,8192]{1,0:T(8,128)(2,1)} %bitcast.57, ...), custom_call_target="tpu_custom_call" | custom-call | tf_op jit(solution)/shard_map/tokens_to_heads/pallas_call | solution.py:125
  68.8 1.2 negate_multiply_fusion
  70.7 1.9 copy.40.rs
  75.3 14.4 %local_states.1 = (bf16[512,256]{1,0:T(8,128)(2,1)}, bf16[512,256]{1,0:T(8,128)(2,1)}, bf16[256,512]{1,0:T(8,128)(2,1)}, bf16[256,512]{1,0:T(8,128)(2,1)}, f32[3...) custom-call(bf16[512,2048]{1,0:T(8,128)(2,1)} %get-tuple-element.44.x, bf16[16,2048]{1,0:T(8,128)(2,1)} %broadcast_select_fusion.xh, ...), custom_call_target="tpu_custom_call" | custom-call | tf_op jit(solution)/shard_map/local_states/pallas_call | solution.py:223
  90.2 0.7 broadcast_in_dim.70.decay
  90.8 77.2 %state_chains.1 = (bf16[32,128,128]{2,1,0:T(8,128)(2,1)}, bf16[32,128,128]{2,1,0:T(8,128)(2,1)}) custom-call(f32[32,128,128]{2,1,0:T(8,128)} %get-tuple-element.56.sl, f32[32,128,128]{2,1,0:T(8,128)} %get-tuple-element.57.dl, f32[32,8,128]{2,1,0:T(8,128)} %broadcast_in_dim.70.decay), custom_call_target="tpu_custom_call" | custom-call | tf_op jit(solution)/shard_map/state_chains/pallas_call | solution.py:286
  168.1 0.7 pad.8.rt
  169.6 46.2 %outputs_and_gradients.1 = (bf16[512,2048]{1,0:T(8,128)(2,1)}, bf16[512,2048]{1,0:T(8,128)(2,1)}, f32[16,2048]{1,0:T(8,128)}, f32[8,2048]{1,0:T(8,128)}, f32[8,2...) custom-call(bf16[512,2048]{1,0:T(8,128)(2,1)} %get-tuple-element.44., ...), custom_call_target="tpu_custom_call" | custom-call | tf_op jit(solution)/shard_map/outputs_and_gradients/pallas_call | solution.py:445
  215.8 0.9 pad_maximum_fusion.1
  216.7 0.8 slice.48
  217.7 1.3 fusion
  219.2 1.4 fusion.7
  221.4 43.5 %small_sums.1 = f32[4,128,128]{2,1,0:T(8,128)} custom-call(f32[128,128]{1,0:T(8,128)} %select_maximum_fusion.v), custom_call_target="tpu_custom_call" | custom-call | tf_op jit(solution)/shard_map/small_sums/pallas_call | solution.py:652
  264.9 1.0 slice.53
  265.9 0.7 pad_maximum_fusion.2
  266.7 0.7 slice.64
  267.3 0.7 slice_reduce_fusion.2
  270.1 61.8 %heads_to_tokens.1 = (bf16[128,8192]{1,0:T(8,128)(2,1)}, bf16[128,8192]{1,0:T(8,128)(2,1)}, bf16[128,1024]{1,0:T(8,128)(2,1)}, bf16[128,1024]{1,0:T(8,128)(2,1)}, bf16[128,128]{1,0:T(8,128)(2,1)}) custom-call(bf16[512,2048]{1,0:T(8,128)(2,1)} %get-tuple-element.60.yf, bf16[512,2048]{1,0:T(8,128)(2,1)} %get-tuple-element.61.gx, ...), custom_call_target="tpu_custom_call" | custom-call | tf_op jit(solution)/shard_map/heads_to_tokens/pallas_call | solution.py:572
  331.9 3.2 copy.53
  335.2 1.3 copy.54
  336.5 0.7 copy.55
  337.2 0.7 copy.56
  (66 shorter events, 8.4 us)
Async XLA Ops:
  68.8 3.9 %copy-start.5 = (f32[4,10240]{1,0:T(4,128)S(1)}, f32[4,10240]{1,0:T(4,128)}, u32[]{:S(2)}) copy-start(f32[4,10240]{1,0:T(4,128)} %param.14) | copy-start | bytes 491524
  68.8 3.9 %copy-start.7 = (f32[10240]{0:T(1024)S(1)}, f32[10240]{0:T(1024)}, u32[]{:S(2)}) copy-start(f32[10240]{0:T(1024)} %param.15) | copy-start | bytes 122884
  70.0 4.0 %copy-start.9 = (bf16[16,256]{1,0:T(8,128)(2,1)S(1)}, bf16[16,256]{1,0:T(8,128)(2,1)}, u32[]{:S(2)}) copy-start(bf16[16,256]{1,0:T(8,128)(2,1)} %get-tuple-element.48) | copy-start | bytes 24580
  70.0 4.0 %copy-start.10 = (bf16[16,256]{1,0:T(8,128)(2,1)S(1)}, bf16[16,256]{1,0:T(8,128)(2,1)}, u32[]{:S(2)}) copy-start(bf16[16,256]{1,0:T(8,128)(2,1)} %get-tuple-element.50) | copy-start | bytes 24580
  70.0 4.6 %copy-start.6 = (bf16[16,2048]{1,0:T(8,128)(2,1)S(1)}, bf16[16,2048]{1,0:T(8,128)(2,1)}, u32[]{:S(2)}) copy-start(bf16[16,2048]{1,0:T(8,128)(2,1)} %get-tuple-element.45) | copy-start | bytes 196612
  90.8 77.9 %copy-start.11 = (f32[128]{0:T(128)S(1)}, f32[128]{0:T(128)}, u32[]{:S(2)}) copy-start(f32[128]{0:T(128)} %param.18) | copy-start | bytes 1540
  169.6 49.6 %copy-start.2 = (bf16[512,128]{1,0:T(8,128)(2,1)S(1)}, bf16[512,128]{1,0:T(8,128)(2,1)}, u32[]{:S(2)}) copy-start(bf16[512,128]{1,0:T(8,128)(2,1)} %get-tuple-element.51) | copy-start | bytes 393220
  269.4 0.7 copy-start.1
  331.9 3.3 copy-start
  335.2 1.3 copy-start.4
  335.2 2.0 copy-start.3
  335.2 2.7 copy-start.8

commit v2 on v1

--- a/solution.py
+++ b/solution.py
@@ -234,7 +234,7 @@
     )(x, xh, dy, w, b, bh, c, ch, wb, wc, rs)
 
 
-STEP = 3
+STEP = 5
 
 
 def chain_kernel(sl, dl, decay, so, do, sbuf, dbuf, ss, sr, ds, dr):
@@ -297,10 +297,24 @@
     )(sl, dl, decay)
 
 
+WW = XW + 2 * N
+VW = 3072
+ZW = VW // 8
+
+
 def join(ref):
     return jnp.concatenate(
         [jnp.concatenate([ref[2 * i], ref[2 * i + 1]], axis=1) for i in range(2)], axis=0
     ).astype(F32)
+
+
+def pieces(q, count):
+    out = []
+    for _ in range(count):
+        hi = q.astype(BF)
+        out.append(hi)
+        q = q - hi.astype(F32)
+    return out
 
 
 def conv_back(pad, dpad, w, out, last, corr, dw):
@@ -326,21 +340,86 @@
     dw[...] = jnp.concatenate(sums + [z] * 3, axis=0)
 
 
-def final_kernel(x, xh, dy, w, b, bh, c, ch, wb, wc, rs, rt, skip, bc, cc, bct, cct, sin, din,
-                 yo, gxo, xlast, xcorr, xdw, gbo, blast, bcorr, bdw, gco, clast, ccorr, cdw, qo, dso,
-                 pad, dpad, S, sc, gacc, db, dc):
+def final_kernel(x, xh, dy, w, b, bh, c, ch, wb, wc, rs, rt, skip, bc, cc, bct, cct, sin, din, logs, sig, rate,
+                 yo, gxo, gbo, gco, gdo, toto,
+                 pad, dpad, S, sc, gacc, db, dc, qs, ends_s,
+                 ybuf, gbuf, bbuf, cbuf, last, corr, halo, tail, gdt, dts, v, ra, rb, part, mid, tot,
+                 xs, xr, bs, br, gs, gr, ks, kr, ts, tr, loc, s1, r1, s2, r2, s3, r3):
     pid = pl.program_id(0)
+    dp_i = lax.axis_index("dp")
+    me, y, seg = place()
+    base = seg * NY
+    xhi = lax.div(seg, 8)
+    z = lax.rem(seg, 8)
+    up = lax.rem(seg + 1, NSEG) * NY + y
+    down = lax.rem(seg + NSEG - 1, NSEG) * NY + y
+    hops = (1, 3, 2)
+    peers = [base + lax.rem(y + i, NY) for i in hops]
+
+    def to(d, h, zz, yy):
+        return {"dp": d, "sp": h * 32 + zz * 4 + yy}
+
+    along_z = [to(dp_i, xhi, lax.rem(z + i, 8), y) for i in range(1, 8)]
+    pos = dp_i * 2 + xhi
+    along_x = []
+    for i in range(1, 8):
+        q = lax.rem(pos + i, 8)
+        along_x.append(to(lax.div(q, 2), lax.rem(q, 2), z, y))
+    pzy = z * 4 + y
+    along_zy = [{"dp": dp_i, "sp": xhi * 32 + lax.rem(pzy + i, 32)} for i in range(1, 32)]
+
+    def lanes(i, wd):
+        return pl.ds(pl.multiple_of(i * wd, wd), wd)
+
+    def bulk(i, act):
+        for k, hop in enumerate(hops):
+            j = lax.rem(y + hop, NY)
+            dst_l = pl.ds(pl.multiple_of(y * XW + i * CW, CW), CW)
+            act(remote(ybuf.at[pl.ds(pl.multiple_of(j * Q, Q), Q), lanes(i, CW)], yo.at[:, dst_l],
+                       xs.at[i, 0, k], xr.at[i, 0, k], peers[k]))
+            for rows, cond in ((Q - 16, j == NY - 1), (Q, j != NY - 1)):
+                @pl.when(cond)
+                def _():
+                    act(remote(gbuf.at[pl.ds(pl.multiple_of(j * Q, Q), rows), lanes(i, CW)],
+                               gxo.at[pl.ds(0, rows), dst_l], xs.at[i, 1, k], xr.at[i, 1, k], peers[k]))
+
+    def bulk_wait(i):
+        src_l = lanes(i, CW)
+        for k in range(3):
+            remote(ybuf.at[pl.ds(0, Q), src_l], yo.at[:, src_l], xs.at[i, 0, k], xr.at[i, 0, k], peers[k]).wait_recv()
+            for rows, cond in ((Q - 16, y == NY - 1), (Q, y != NY - 1)):
+                @pl.when(cond)
+                def _():
+                    remote(gbuf.at[pl.ds(0, rows), src_l], gxo.at[pl.ds(0, rows), src_l],
+                           xs.at[i, 1, k], xr.at[i, 1, k], peers[k]).wait_recv()
+
+    def halo_copy(i):
+        return remote(corr.at[:, lanes(i, CW)], halo.at[:, lanes(i, CW)], ks.at[i], kr.at[i], down)
 
     @pl.when(pid == 0)
     def _():
+        barrier = pltpu.get_barrier_semaphore()
+        for t in along_x + along_zy:
+            pl.semaphore_signal(barrier, inc=1, device_id=t, device_id_type=MESH)
+        for t in (up, down):
+            pl.semaphore_signal(barrier, inc=1, device_id={"sp": t}, device_id_type=MESH)
+        pl.semaphore_wait(barrier, 40)
         for k in range(NB):
             sl = slice(k * Q, (k + 1) * Q)
             sc[k] = dot(cc[sl, :], bc[sl, :], 1, 1)
         gacc[...] = jnp.zeros_like(gacc)
         db[...] = jnp.zeros_like(db)
         dc[...] = jnp.zeros_like(dc)
-        qo[...] = jnp.zeros_like(qo)
-
+        qs[...] = jnp.zeros_like(qs)
+        ends_s[...] = jnp.zeros_like(ends_s)
+        v[...] = jnp.zeros_like(v)
+
+    @pl.when(pid > 0)
+    def _():
+        bulk(pid - 1, lambda cp: cp.start())
+        halo_copy(pid - 1).start()
+
+    here = lanes(pid, CW)
     fill(pad, xh, x)
     wx = w[...]
     S[0] = join(sin)
@@ -357,8 +436,8 @@
     D = join(din)
     causal = lax.broadcasted_iota(jnp.int32, (Q, Q), 0) >= lax.broadcasted_iota(jnp.int32, (Q, Q), 1)
     low = lax.broadcasted_iota(jnp.int32, (Q, 128), 1) < 64
-    er = lax.broadcasted_iota(jnp.int32, (CW, 128), 0) // 64 + pid * (CW // 64)
-    el = lax.broadcasted_iota(jnp.int32, (CW, 128), 1)
+    er = lax.broadcasted_iota(jnp.int32, (CW, 128), 0) // 64 + pid * (CW // 64) + y * (XW // 64)
+    pick = (lax.broadcasted_iota(jnp.int32, (CW, 128), 1) == er).astype(BF)
     ends = []
     for k in reversed(range(NB)):
         sl = slice(k * Q, (k + 1) * Q)
@@ -376,14 +455,14 @@
         ee = jnp.exp(re - r)
         ub = (xc * st).astype(BF)
         wt = (xc * (st * ee)).astype(BF)
-        v = (dyf * er_).astype(BF)
+        vv = (dyf * er_).astype(BF)
         Sb = S[k].astype(BF)
         Db = D.astype(BF)
         ends.append(jnp.sum(D * S[k + 1], axis=0, keepdims=True))
         ya = er_ * dot(cc[sl, :], Sb, 1, 0)
         du = ee * dot(bc[sl, :], Db, 1, 0)
         db[sl, :] += dot(wt, Db, 1, 1)
-        dc[sl, :] += dot(v, Sb, 1, 1)
+        dc[sl, :] += dot(vv, Sb, 1, 1)
         yw, dw_ = [], []
         g = sc[k]
         acc = gacc[k]
@@ -393,279 +472,209 @@
             for h in (2 * p, 2 * p + 1):
                 gap = rc[:, h : h + 1] - rt[0, h : h + 1, sl]
                 ls.append(jnp.exp(jnp.where(causal, gap, -1e30)))
-            up = ub[:, p * 128 : (p + 1) * 128]
-            dp = dyb[:, p * 128 : (p + 1) * 128]
-            ublk = jnp.concatenate([jnp.where(low, up, zero), jnp.where(low, zero, up)], axis=0)
-            dblk = jnp.concatenate([jnp.where(low, dp, zero), jnp.where(low, zero, dp)], axis=0)
+            u2 = ub[:, p * 128 : (p + 1) * 128]
+            d2 = dyb[:, p * 128 : (p + 1) * 128]
+            ublk = jnp.concatenate([jnp.where(low, u2, zero), jnp.where(low, zero, u2)], axis=0)
+            dblk = jnp.concatenate([jnp.where(low, d2, zero), jnp.where(low, zero, d2)], axis=0)
             ms = [(g * l).astype(BF) for l in ls]
             yw.append(dot(jnp.concatenate(ms, axis=1), ublk, 1, 0))
             dw_.append(dot(jnp.concatenate(ms, axis=0), dblk, 0, 0))
-            dm = dot(dp, ublk, 1, 1)
+            dm = dot(d2, ublk, 1, 1)
             acc = acc + dm[:, :Q] * ls[0] + dm[:, Q:] * ls[1]
         gacc[k] = acc
         yin = ya + jnp.concatenate(yw, axis=1)
         du = du + jnp.concatenate(dw_, axis=1)
         sk = skip[0:1, :]
-        yo[sl, :] = (yin + sk * xc).astype(BF)
-        qs = (dyf * yin - ub.astype(F32) * du, xc * du, dyf * xc)
-        total = jnp.zeros((Q, 128), F32)
-        for i, q in enumerate(qs):
-            e = (el == er + 32 * i).astype(BF)
-            hi = q.astype(BF)
-            lo = (q - hi.astype(F32)).astype(BF)
-            total = total + dot(hi, e, 1, 0) + dot(lo, e, 1, 0)
-        qo[sl, :] += total
+        ybuf[sl, here] = (yin + sk * xc).astype(BF)
+        for i, q in enumerate((dyf * yin - ub.astype(F32) * du, xc * du, dyf * xc)):
+            parts = pieces(q, 2)
+            qs[i, sl, :] += dot(parts[0], pick, 1, 0) + dot(parts[1], pick, 1, 0)
         gx = st * du + sk * dyf
         dpad[sl, :] = gx * (sg * (1.0 + s * (1.0 - sg)))
-        D = jnp.exp(re) * D + dot(cct[:, sl], v, 1, 0)
-    dso[...] = jnp.concatenate(ends[::-1] + [jnp.zeros((4, CW), F32)], axis=0)
-    conv_back(pad, dpad, wx, gxo, xlast, xcorr, xdw)
+        D = jnp.exp(re) * D + dot(cct[:, sl], vv, 1, 0)
+    for part_e in pieces(jnp.concatenate(ends[::-1] + [jnp.zeros((4, CW), F32)], axis=0), 3):
+        ends_s[...] += dot(part_e, pick, 1, 0)
+    conv_back(pad, dpad, wx, gbuf.at[:, here], last.at[:, here], corr.at[:, here], v.at[:, here])
 
     @pl.when(pid == NCH - 1)
     def _():
-        for raw, halo, wt, gout, lst, crr, dwo, acc, other, tr in (
-            (b, bh, wb, gbo, blast, bcorr, bdw, db, cc, True),
-            (c, ch, wc, gco, clast, ccorr, cdw, dc, bc, False),
+        for raw, hal, wt, gout, at, acc, other, tr_ in (
+            (b, bh, wb, bbuf, XW, db, cc, True),
+            (c, ch, wc, cbuf, XW + N, dc, bc, False),
         ):
-            fill(pad, halo, raw)
+            fill(pad, hal, raw)
             for k in range(NB):
                 sl = slice(k * Q, (k + 1) * Q)
                 gk = gacc[k].astype(BF)
-                tot = acc[sl, :] + dot(gk, other[sl, :], 0 if tr else 1, 0)
+                tt = acc[sl, :] + dot(gk, other[sl, :], 0 if tr_ else 1, 0)
                 s = conv_rows(pad, wt[...], wt[4:5, :], k)
                 sg = sigmoid(s)
-                dpad[sl, :] = tot * (sg * (1.0 + s * (1.0 - sg)))
-            conv_back(pad, dpad, wt[...], gout, lst, crr, dwo)
-
-
-def finals(x, xh, dy, w, b, bh, c, ch, wb, wc, rs, rt, skip, bc, cc, bct, cct, sin, din):
+                dpad[sl, :] = tt * (sg * (1.0 + s * (1.0 - sg)))
+            ln = slice(at, at + N)
+            conv_back(pad, dpad, wt[...], gout, last.at[:, ln], corr.at[:, ln], v.at[:, ln])
+        after = (lax.broadcasted_iota(jnp.int32, (Q, Q), 0) <= lax.broadcasted_iota(jnp.int32, (Q, Q), 1)).astype(BF)
+        own = lax.broadcasted_iota(jnp.int32, (1, 128), 1) // (XW // 64) == y
+        sums = [jnp.zeros((1, 128), F32) for _ in range(3)]
+        for k in range(NB):
+            sl = slice(k * Q, (k + 1) * Q)
+            dlog = ends_s[k : k + 1, :] + sum(dot(after, p, 1, 0) for p in pieces(qs[0, sl, :], 3))
+            draw = (qs[1, sl, :] - dlog * rate[0:1, :]) * sig[sl, :]
+            gdt[sl, :] = draw.astype(BF)
+            for i, q in enumerate((dlog * logs[sl, :], draw, qs[2, sl, :])):
+                sums[i] = sums[i] + jnp.sum(q, axis=0, keepdims=True)
+        v[:, WW : WW + 128] = jnp.where(own, jnp.concatenate(sums + [jnp.zeros((5, 128), F32)], axis=0), 0.0)
+
+        bulk(NCH - 1, lambda cp: cp.start())
+        for i in range(NCH - 1, NCH + 2):
+            halo_copy(i).start()
+
+        def side(act):
+            for k, hop in enumerate(hops):
+                j = lax.rem(y + hop, NY)
+                act(remote(gdt.at[pl.ds(pl.multiple_of(j * Q, Q), Q), :], dts.at[k], gs.at[k], gr.at[k], peers[k]))
+                for n, (src, dst) in enumerate(((bbuf, gbo), (cbuf, gco))):
+                    for rows, cond in ((Q - 16, j == NY - 1), (Q, j != NY - 1)):
+                        @pl.when(cond)
+                        def _():
+                            act(remote(src.at[pl.ds(pl.multiple_of(j * Q, Q), rows), :],
+                                       dst.at[pl.ds(0, rows), lanes(y, N)], bs.at[n, k], br.at[n, k], peers[k]))
+
+        side(lambda cp: cp.start())
+
+        def send(src, dst, sa, sb, t):
+            cp = pltpu.make_async_remote_copy(src_ref=src, dst_ref=dst, send_sem=sa, recv_sem=sb,
+                                              device_id=t, device_id_type=MESH)
+            cp.start()
+            return cp
+
+        first = [send(v.at[:, lanes(lax.rem(z + i + 1, 8), ZW)], ra.at[z], s1.at[i], r1.at[i], t)
+                 for i, t in enumerate(along_z)]
+        mine = pl.ds(pl.multiple_of(y * Q, Q), Q)
+        y_own = pltpu.make_async_copy(ybuf.at[mine, :], yo.at[:, lanes(y, XW)], loc.at[0])
+        y_own.start()
+        for i in range(NCH + 2):
+            halo_copy(i).wait_recv()
+
+        @pl.when(seg == NSEG - 1)
+        def _():
+            tail[...] = last[...].astype(BF)
+
+        @pl.when(seg != NSEG - 1)
+        def _():
+            tail[0:8, :] = last[0:8, :].astype(BF)
+            tail[8:16, :] = (last[8:16, :] + halo[...]).astype(BF)
+
+        tails = ((0, XW, gxo), (XW, N, gbo), (XW + N, N, gco))
+
+        def tail_copy(n, k):
+            at, wd, dst = tails[n]
+            return remote(tail.at[:, pl.ds(at, wd)], dst.at[pl.ds(Q - 16, 16), lanes(y, wd)],
+                          ts.at[n, k], tr.at[n, k], base + NY - 1)
+
+        for k, hop in enumerate(hops):
+            @pl.when(lax.rem(y + hop, NY) == NY - 1)
+            def _():
+                for n in range(3):
+                    tail_copy(n, k).start()
+
+        @pl.when(y == NY - 1)
+        def _():
+            gbuf[T - 16 :, :] = tail[:, :XW]
+            bbuf[T - 16 :, :] = tail[:, XW : XW + N]
+            cbuf[T - 16 :, :] = tail[:, XW + N :]
+
+        ra[z] = v[:, lanes(z, ZW)]
+        for cp in first:
+            cp.wait()
+        t1 = ra[0]
+        for i in range(1, 8):
+            t1 = t1 + ra[i]
+        part[...] = t1
+        rb[pos] = t1
+        second = [send(part, rb.at[pos], s2.at[i], r2.at[i], t) for i, t in enumerate(along_x)]
+        owns = [y_own]
+        for n, (src, dst, wd) in enumerate(((gbuf, gxo, XW), (bbuf, gbo, N), (cbuf, gco, N))):
+            o = pltpu.make_async_copy(src.at[mine, :], dst.at[:, lanes(y, wd)], loc.at[1 + n])
+            o.start()
+            owns.append(o)
+        for cp in second:
+            cp.wait()
+        t2 = rb[0]
+        for i in range(1, 8):
+            t2 = t2 + rb[i]
+        mid[...] = t2
+        zl = lanes(z, ZW)
+        tot[y, :, zl] = t2
+        third = [send(mid, tot.at[y, :, zl], s3.at[i], r3.at[i], t) for i, t in enumerate(along_zy)]
+        for cp in third:
+            cp.wait()
+        toto[...] = tot[...]
+        side(lambda cp: cp.wait_send())
+        for k in range(3):
+            remote(gdt.at[pl.ds(0, Q), :], dts.at[k], gs.at[k], gr.at[k], peers[k]).wait_recv()
+            for n, (src, dst) in enumerate(((bbuf, gbo), (cbuf, gco))):
+                for rows, cond in ((Q - 16, y == NY - 1), (Q, y != NY - 1)):
+                    @pl.when(cond)
+                    def _():
+                        remote(src.at[pl.ds(0, rows), :], dst.at[pl.ds(0, rows), pl.ds(0, N)],
+                               bs.at[n, k], br.at[n, k], peers[k]).wait_recv()
+        gd = gdt[mine, :].astype(F32)
+        for k in range(3):
+            gd = gd + dts[k].astype(F32)
+        gdo[...] = gd.astype(BF)
+        for o in owns:
+            o.wait()
+        for i in range(NCH + 2):
+            halo_copy(i).wait_send()
+
+        def drain(i, carry):
+            bulk(i, lambda cp: cp.wait_send())
+            bulk_wait(i)
+            return carry
+
+        lax.fori_loop(0, NCH, drain, 0)
+        for k, hop in enumerate(hops):
+            @pl.when(lax.rem(y + hop, NY) == NY - 1)
+            def _():
+                for n in range(3):
+                    tail_copy(n, k).wait_send()
+
+            @pl.when(y == NY - 1)
+            def _():
+                for n in range(3):
+                    tail_copy(n, k).wait_recv()
+
+
+def finals(*args):
     s = jax.ShapeDtypeStruct
-    bx = [whole(T, N), whole(16, N), whole(8, N), whole(8, N)]
-    bs = [s((T, N), BF), s((16, N), F32), s((8, N), F32), s((8, N), F32)]
+    V = pltpu.VMEM
+    dma = pltpu.SemaphoreType.DMA
     return pl.pallas_call(
         final_kernel,
         name="outputs_and_gradients",
         grid=(NCH,),
-        out_shape=[s((T, XW), BF), s((T, XW), BF), s((16, XW), F32), s((8, XW), F32), s((8, XW), F32)]
-        + bs + bs + [s((T, 128), F32), s((8, XW), F32)],
+        out_shape=[s((Q, NY * XW), BF), s((Q, NY * XW), BF), s((Q, NY * N), BF), s((Q, NY * N), BF),
+                   s((Q, 128), BF), s((NY, 8, VW), F32)],
         in_specs=[chunked(T), chunked(HALO), chunked(T), chunked(8), whole(T, N), whole(HALO, N),
                   whole(T, N), whole(HALO, N), whole(8, N), whole(8, N), RS, RT, chunked(8),
-                  whole(T, N), whole(T, N), whole(N, T), whole(N, T), PIECES, PIECES],
-        out_specs=[chunked(T), chunked(T), chunked(16), chunked(8), chunked(8)] + bx + bx
-        + [whole(T, 128), chunked(8)],
+                  whole(T, N), whole(T, N), whole(N, T), whole(N, T), PIECES, PIECES,
+                  whole(T, 128), whole(T, 128), whole(8, 128)],
+        out_specs=[ANY] * 4 + [whole(Q, 128), whole(NY, 8, VW)],
         scratch_shapes=[
-            pltpu.VMEM((T + 8, CW), F32),
-            pltpu.VMEM((T + 8, CW), F32),
-            pltpu.VMEM((NB + 1, N, CW), F32),
-            pltpu.VMEM((NB, Q, Q), F32),
-            pltpu.VMEM((NB, Q, Q), F32),
-            pltpu.VMEM((T, N), F32),
-            pltpu.VMEM((T, N), F32),
+            V((T + 8, CW), F32), V((T + 8, CW), F32), V((NB + 1, N, CW), F32),
+            V((NB, Q, Q), F32), V((NB, Q, Q), F32), V((T, N), F32), V((T, N), F32),
+            V((3, T, 128), F32), V((8, 128), F32),
+            V((T, XW), BF), V((T, XW), BF), V((T, N), BF), V((T, N), BF),
+            V((16, WW), F32), V((8, WW), F32), V((8, WW), F32), V((16, WW), BF),
+            V((T, 128), BF), V((3, Q, 128), BF),
+            V((8, VW), F32), V((8, 8, ZW), F32), V((8, 8, ZW), F32), V((8, ZW), F32), V((8, ZW), F32),
+            V((NY, 8, VW), F32),
+            dma((NCH, 2, 3)), dma((NCH, 2, 3)), dma((2, 3)), dma((2, 3)), dma((3,)), dma((3,)),
+            dma((NCH + 2,)), dma((NCH + 2,)), dma((3, 3)), dma((3, 3)), dma((4,)),
+            dma((7,)), dma((7,)), dma((7,)), dma((7,)), dma((31,)), dma((31,)),
         ],
-        compiler_params=pltpu.CompilerParams(vmem_limit_bytes=VLIM),
-    )(x, xh, dy, w, b, bh, c, ch, wb, wc, rs, rt, skip, bc, cc, bct, cct, sin, din)
-
-
-def give_kernel(yf, gx, gb, gc, gdt, lx, lb, lc, kx, kb, kc,
-                yo, gxo, gbo, gco, gdo,
-                stage, stage_s, hx, hb, hc, tx, tb, tc, dts, send, recv, ks, kr, ts, tr, loc):
-    me, y, seg = place()
-    base = seg * NY
-    up = lax.rem(seg + 1, NSEG) * NY + y
-    down = lax.rem(seg + NSEG - 1, NSEG) * NY + y
-    peers = [base + lax.rem(y + i, NY) for i in (1, 3, 2)]
-    barrier = greet(peers + [up, down])
-    pl.semaphore_wait(barrier, 5)
-    halos = [remote(src, dst, ks.at[n], kr.at[n], down) for n, (src, dst) in enumerate(((kx, hx), (kb, hb), (kc, hc)))]
-    for cp in halos:
-        cp.start()
-
-    def cols(w):
-        return pl.ds(pl.multiple_of(y * w, w), w)
-
-    arrays = ((yf, yo, XW, Q), (gx, gxo, XW, Q - 16), (gb, gbo, N, Q - 16), (gc, gco, N, Q - 16))
-    copies = []
-    for n, (src, dst, w, rows) in enumerate(arrays):
-        for i, k in enumerate((1, 3, 2)):
-            j = lax.rem(y + k, NY)
-            rs = pl.ds(pl.multiple_of(j * Q, Q), rows)
-            cp = remote(src.at[rs, :], dst.at[pl.ds(0, rows), cols(w)], send.at[n, i], recv.at[n, i], peers[i])
-            cp.start()
-            copies.append(cp)
-    for i, k in enumerate((1, 3, 2)):
-        j = lax.rem(y + k, NY)
-        rs = pl.ds(pl.multiple_of(j * Q, Q), Q)
-        cp = remote(gdt.at[rs, :], dts.at[i], send.at[4, i], recv.at[4, i], peers[i])
-        cp.start()
-        copies.append(cp)
-    mine = pl.ds(pl.multiple_of(y * Q, Q), Q)
-    tails = ((gx, gxo, XW, tx), (gb, gbo, N, tb), (gc, gco, N, tc))
-    for n, (cp, t, l, h) in enumerate(zip(halos, (tx, tb, tc), (lx, lb, lc), (hx, hb, hc))):
-        cp.wait_recv()
-
-        @pl.when(seg == NSEG - 1)
-        def _():
-            t[...] = l[...].astype(BF)
-
-        @pl.when(seg != NSEG - 1)
-        def _():
-            t[0:8, :] = l[0:8, :].astype(BF)
-            t[8:16, :] = (l[8:16, :] + h[...]).astype(BF)
-
-    def tail(n, i, k, do):
-        src, dst, w, t = tails[n]
-        j = lax.rem(y + k, NY)
-        place_to = dst.at[pl.ds(Q - 16, 16), cols(w)]
-
-        @pl.when(j == NY - 1)
-        def _():
-            do(remote(t, place_to, ts.at[n, i], tr.at[n, i], peers[i]))
-
-        @pl.when(j != NY - 1)
-        def _():
-            rs = pl.ds(pl.multiple_of(j * Q + Q - 16, 16), 16)
-            do(remote(src.at[rs, :], place_to, ts.at[n, i], tr.at[n, i], peers[i]))
-
-    for n in range(3):
-        for i, k in enumerate((1, 3, 2)):
-            tail(n, i, k, lambda cp: cp.start())
-    ins = []
-    for n, (src, dst, w, rows) in enumerate(arrays):
-        st = stage.at[n] if w == XW else stage_s.at[n - 2]
-        cp = pltpu.make_async_copy(src.at[mine, :], st, loc.at[n])
-        cp.start()
-        ins.append((cp, st, dst, w))
-    outs = []
-    for n, (cp, st, dst, w) in enumerate(ins):
-        cp.wait()
-        if n > 0:
-            t = tails[n - 1][3]
-
-            @pl.when(y == NY - 1)
-            def _():
-                st[Q - 16 :, :] = t[...]
-
-        o = pltpu.make_async_copy(st, dst.at[:, cols(w)], loc.at[4 + n])
-        o.start()
-        outs.append(o)
-    own = pltpu.make_async_copy(gdt.at[mine, :], dts.at[3], loc.at[8])
-    own.start()
-    own.wait()
-    for cp in copies[12:]:
-        cp.wait_recv()
-    gdo[...] = (dts[0].astype(F32) + dts[1].astype(F32) + dts[2].astype(F32) + dts[3].astype(F32)).astype(BF)
-    for o in outs:
-        o.wait()
-    for cp in copies[:12]:
-        cp.wait_recv()
-    for n in range(3):
-        for i, k in enumerate((1, 3, 2)):
-            tail(n, i, k, lambda cp: cp.wait())
-    for cp in copies:
-        cp.wait_send()
-    for cp in halos:
-        cp.wait_send()
-
-
-def give(*args):
-    s = jax.ShapeDtypeStruct
-    return pl.pallas_call(
-        give_kernel,
-        name="heads_to_tokens",
-        out_shape=(s((Q, NY * XW), BF), s((Q, NY * XW), BF), s((Q, NY * N), BF), s((Q, NY * N), BF), s((Q, 128), BF)),
-        in_specs=[ANY] * 5 + [VM] * 6,
-        out_specs=[ANY] * 4 + [VM],
-        scratch_shapes=[
-            pltpu.VMEM((2, Q, XW), BF),
-            pltpu.VMEM((2, Q, N), BF),
-            pltpu.VMEM((8, XW), F32), pltpu.VMEM((8, N), F32), pltpu.VMEM((8, N), F32),
-            pltpu.VMEM((16, XW), BF), pltpu.VMEM((16, N), BF), pltpu.VMEM((16, N), BF),
-            pltpu.VMEM((4, Q, 128), BF),
-            pltpu.SemaphoreType.DMA((5, 3)),
-            pltpu.SemaphoreType.DMA((5, 3)),
-            pltpu.SemaphoreType.DMA((3,)),
-            pltpu.SemaphoreType.DMA((3,)),
-            pltpu.SemaphoreType.DMA((3, 3)),
-            pltpu.SemaphoreType.DMA((3, 3)),
-            pltpu.SemaphoreType.DMA((9,)),
-        ],
-        compiler_params=pltpu.CompilerParams(collective_id=2, has_side_effects=True),
+        compiler_params=pltpu.CompilerParams(collective_id=2, has_side_effects=True, vmem_limit_bytes=VLIM),
     )(*args)
-
-
-def total_kernel(v, out, ra, rb, part, mid, s1, r1, s2, r2, s3, r3):
-    dp = lax.axis_index("dp")
-    me, y, seg = place()
-    xh = lax.div(seg, 8)
-    z = lax.rem(seg, 8)
-
-    def to(d, h, zz, yy):
-        return {"dp": d, "sp": h * 32 + zz * 4 + yy}
-
-    along_z = [to(dp, xh, lax.rem(z + i, 8), y) for i in range(1, 8)]
-    pos = dp * 2 + xh
-    along_x = []
-    for i in range(1, 8):
-        q = lax.rem(pos + i, 8)
-        along_x.append(to(lax.div(q, 2), lax.rem(q, 2), z, y))
-    pzy = z * 4 + y
-    along_zy = []
-    for i in range(1, 32):
-        q = lax.rem(pzy + i, 32)
-        along_zy.append({"dp": dp, "sp": xh * 32 + q})
-    barrier = pltpu.get_barrier_semaphore()
-    for t in along_x + along_zy:
-        pl.semaphore_signal(barrier, inc=1, device_id=t, device_id_type=MESH)
-    pl.semaphore_wait(barrier, 38)
-
-    def send(src, dst, a, b, t):
-        cp = pltpu.make_async_remote_copy(src_ref=src, dst_ref=dst, send_sem=a, recv_sem=b, device_id=t, device_id_type=MESH)
-        cp.start()
-        return cp
-
-    def block(i):
-        return pl.ds(pl.multiple_of(i * 16, 16), 16)
-
-    first = [send(v.at[block(lax.rem(z + i + 1, 8)), :], ra.at[z], s1.at[i], r1.at[i], t) for i, t in enumerate(along_z)]
-    ra[z] = v[block(z), :]
-    for cp in first:
-        cp.wait()
-    tot = ra[0]
-    for i in range(1, 8):
-        tot = tot + ra[i]
-    part[...] = tot
-    rb[pos] = tot
-    second = [send(part, rb.at[pos], s2.at[i], r2.at[i], t) for i, t in enumerate(along_x)]
-    for cp in second:
-        cp.wait()
-    tot = rb[0]
-    for i in range(1, 8):
-        tot = tot + rb[i]
-    mid[...] = tot
-    out[y, block(z), :] = tot
-    third = [send(mid, out.at[y, block(z), :], s3.at[i], r3.at[i], t) for i, t in enumerate(along_zy)]
-    for cp in third:
-        cp.wait()
-
-
-def totals(v):
-    return pl.pallas_call(
-        total_kernel,
-        name="small_sums",
-        out_shape=jax.ShapeDtypeStruct((NY, 128, 128), F32),
-        in_specs=[VM],
-        out_specs=VM,
-        scratch_shapes=[
-            pltpu.VMEM((8, 16, 128), F32),
-            pltpu.VMEM((8, 16, 128), F32),
-            pltpu.VMEM((16, 128), F32),
-            pltpu.VMEM((16, 128), F32),
-            pltpu.SemaphoreType.DMA((7,)), pltpu.SemaphoreType.DMA((7,)),
-            pltpu.SemaphoreType.DMA((7,)), pltpu.SemaphoreType.DMA((7,)),
-            pltpu.SemaphoreType.DMA((31,)), pltpu.SemaphoreType.DMA((31,)),
-        ],
-        compiler_params=pltpu.CompilerParams(collective_id=3, has_side_effects=True),
-    )(v)
 
 
 def per_device(ssm_input, b_input, c_input, dt_input, conv_weight, conv_bias, a_log, dt_bias, skip_gain, grad_out):
@@ -701,27 +710,19 @@
     decay = jnp.broadcast_to(decay, (NPIECE, 8, 128))
     bc, cc, bct, cct, sl, dl = local_states(x, xh, dy, w, b, bh, c, ch, wb, wc, rs)
     sin, din = chains(sl, dl, decay)
-    (yf, gx, xlast, xcorr, xdw, gb, blast, bcorr, bdw, gc, clast, ccorr, cdw, qs, ends) = finals(
-        x, xh, dy, w, b, bh, c, ch, wb, wc, rs, rt, skip, bc, cc, bct, cct, sin, din
+    full = dt.astype(F32) + dt_bias[None, :]
+    full_rate = jnp.exp(a_log)
+    yo, gxo, gbo, gco, gdo, tot = finals(
+        x, xh, dy, w, b, bh, c, ch, wb, wc, rs, rt, skip, bc, cc, bct, cct, sin, din,
+        -jax.nn.softplus(full) * full_rate[None, :], jax.nn.sigmoid(full),
+        jnp.broadcast_to(full_rate[None, :], (8, 128)),
     )
-    q1 = qs[:, :heads].reshape(NB, Q, heads)
-    end = ends[:NB].reshape(NB, heads, 64).sum(-1)
-    dlog = (jnp.einsum("ts,kth->ksh", tril, q1, precision=HP) + end[:, None, :]).reshape(T, heads)
-    dstep = qs[:, heads : 2 * heads] - dlog * rate[None, :]
-    draw = dstep * jax.nn.sigmoid(raw)
-    gdt = jnp.zeros((T, 128), BF)
-    gdt = lax.dynamic_update_slice_in_dim(gdt, draw.astype(BF), y * heads, 1)
-    hg = jnp.stack([(dlog * logs).sum(0), draw.sum(0), qs[:, 2 * heads : 3 * heads].sum(0)])
-    v = jnp.concatenate([xdw[:5], bdw[:5], cdw[:5]], 1).reshape(100, 128)
-    hrow = jnp.pad(hg.reshape(1, 3 * heads), ((0, 27), (0, 128 - 3 * heads)))
-    tot = totals(jnp.concatenate([v, hrow], 0))
-    grads = tot[:, :100, :].reshape(NY, 5, XW + 2 * N).transpose(1, 0, 2)
+    grads = tot[:, :5, :].transpose(1, 0, 2)
     gw = jnp.concatenate(
-        [grads[:, :, :XW].reshape(5, -1), grads[:, :, XW : XW + N].reshape(5, -1), grads[:, :, XW + N :].reshape(5, -1)], 1
+        [grads[:, :, :XW].reshape(5, -1), grads[:, :, XW : XW + N].reshape(5, -1), grads[:, :, XW + N : WW].reshape(5, -1)], 1
     )
-    hsum = tot[:, 100, : 3 * heads].reshape(NY, 3, heads).transpose(1, 0, 2).reshape(3, NY * heads)
+    hsum = tot[:, :3, WW : WW + 128].sum(0)
     hsum = lax.dynamic_slice_in_dim(hsum, me * 2, 2, 1)
-    yo, gxo, gbo, gco, gdo = give(yf, gx, gb, gc, gdt, xlast, blast, clast, xcorr, bcorr, ccorr)
     return (yo[None], gxo[None], gbo[None], gco[None], gdo[None], gw[:4], gw[4], hsum)
 
 

time: 339 us -> 265 us (0.78)
  Pallas kernels: 310 us -> 238 us
    pallas_call x2 -> x0, Pallas kernels: 105 us -> none  [the longest x1 61.8 us: give(): pl.pallas_call(give_kernel, name='heads_to_tokens', out_shape=(s((Q, NY *...]
    pallas_call x1, Pallas kernels: 46.2 us -> 88.6 us  [finals(): pl.pallas_call(final_kernel, name='outputs_and_gradients', grid=(NCH,), o...]
    pallas_call x1, Pallas kernels: 77.2 us -> 68.7 us  [chains(): pl.pallas_call(chain_kernel, name='state_chains', out_shape=(s, s), in_sp...]
    unnamed x30 -> x20, local copies, waits for them, and re-layouts: 7.94 us -> 6.36 us
where the time goes in v2:
time: 265 us; the launch traced here: 263 us
  Pallas kernels  238 us (90%)
  local copies, waits for them, and re-layouts  17.5 us (7%)
  other arithmetic  6.24 us (2%)
    pallas_call x1, Pallas kernels, finals(): pl.pallas_call(final_kernel, name='outputs_and_gradients', grid=(NCH,), o...  88.6 us
    pallas_call x1, Pallas kernels, chains(): pl.pallas_call(chain_kernel, name='state_chains', out_shape=(s, s), in_sp...  68.7 us
    pallas_call x1, Pallas kernels, bring(): pl.pallas_call(bring_kernel, name='tokens_to_heads', out_shape=(s((T, XW)...  66.7 us
    pallas_call x1, Pallas kernels, local_states(): pl.pallas_call(kern, name='local_states', grid=(NCH,), out_shape=(s((T, N...  14.4 us
    unnamed x20, local copies, waits for them, and re-layouts  6.36 us

profile of v2, /device:TPU:1, one launch (start us, length us, event | category | flops | bytes accessed | tf_op | source)
XLA Modules:
  0.0 263.3 jit_solution(1595789505143994673)
XLA Ops:
  0.7 0.7 exp.29
  1.3 0.7 dynamic_slice.30
  2.0 0.7 dynamic-slice_exponential_fusion
  2.8 0.7 dynamic_slice.28
  5.0 1.0 maximum_maximum_fusion
  7.2 66.7 %tokens_to_heads.1 = (bf16[512,2048]{1,0:T(8,128)(2,1)}, bf16[512,2048]{1,0:T(8,128)(2,1)}, bf16[512,256]{1,0:T(8,128)(2,1)}, bf16[512,256]{1,0:T(8,128)(2,1)}, ...) custom-call(bf16[128,8192]{1,0:T(8,128)(2,1)} %bitcast.34, ...), custom_call_target="tpu_custom_call" | custom-call | tf_op jit(solution)/shard_map/tokens_to_heads/pallas_call | solution.py:125
  75.2 1.1 negate_multiply_fusion
  77.5 0.7 broadcast_in_dim.73.decay
  78.2 0.7 pad.4.rt
  78.9 1.0 add_divide_fusion
  79.9 1.9 copy.32.rs
  81.8 14.4 %local_states.1 = (bf16[512,256]{1,0:T(8,128)(2,1)}, bf16[512,256]{1,0:T(8,128)(2,1)}, bf16[256,512]{1,0:T(8,128)(2,1)}, bf16[256,512]{1,0:T(8,128)(2,1)}, f32[3...) custom-call(bf16[512,2048]{1,0:T(8,128)(2,1)} %get-tuple-element.30.x, bf16[16,2048]{1,0:T(8,128)(2,1)} %broadcast_select_fusion.xh, ...), custom_call_target="tpu_custom_call" | custom-call | tf_op jit(solution)/shard_map/local_states/pallas_call | solution.py:223
  96.2 68.7 %state_chains.1 = (bf16[32,128,128]{2,1,0:T(8,128)(2,1)}, bf16[32,128,128]{2,1,0:T(8,128)(2,1)}) custom-call(f32[32,128,128]{2,1,0:T(8,128)} %get-tuple-element.42.sl, f32[32,128,128]{2,1,0:T(8,128)} %get-tuple-element.43.dl, f32[32,8,128]{2,1,0:T(8,128)} %broadcast_in_dim.73.decay), custom_call_target="tpu_custom_call" | custom-call | tf_op jit(solution)/shard_map/state_chains/pallas_call | solution.py:286
  164.9 88.6 %outputs_and_gradients.1 = (bf16[128,8192]{1,0:T(8,128)(2,1)}, bf16[128,8192]{1,0:T(8,128)(2,1)}, bf16[128,1024]{1,0:T(8,128)(2,1)}, bf16[128,1024]{1,0:T(8,128)...) custom-call(bf16[512,2048]{1,0:T(8,128)(2,1)} %get-tuple-element.30.x, bf16[16,2048]{1,0:T(8,128)(2,1)} %broadcast_select_fusion.xh, ...), custom_call_target="tpu_custom_call" | custom-call | tf_op jit(solution)/shard_map/outputs_and_gradients/pallas_call | solution.py:652
  253.6 0.9 slice_reduce_fusion.1
  254.5 0.7 copy.33
  255.2 1.0 slice_bitcast_fusion
  256.2 0.7 pad_maximum_fusion.1
  256.9 0.7 slice.36
  257.6 1.3 copy.40
  259.0 1.0 copy-done
  260.0 1.3 copy.41
  261.3 0.7 copy.42
  262.0 0.7 copy.43
  (40 shorter events, 5.8 us)
Async XLA Ops:
  73.9 4.9 %copy-start.2 = (bf16[512,128]{1,0:T(8,128)(2,1)S(1)}, bf16[512,128]{1,0:T(8,128)(2,1)}, u32[]{:S(2)}) copy-start(bf16[512,128]{1,0:T(8,128)(2,1)} %get-tuple-element.37) | copy-start | bytes 393220
  74.0 4.9 %copy-start.6 = (f32[128]{0:T(128)S(1)}, f32[128]{0:T(128)}, u32[]{:S(2)}) copy-start(f32[128]{0:T(128)} %param.17) | copy-start | bytes 1540
  253.6 4.1 %copy-start.1 = (bf16[128,8192]{1,0:T(8,128)(2,1)S(1)}, bf16[128,8192]{1,0:T(8,128)(2,1)}, u32[]{:S(2)}) copy-start(bf16[128,8192]{1,0:T(8,128)(2,1)} %get-tuple-element.46) | copy-start | bytes 6291460
  257.6 2.3 copy-start
  260.0 1.3 copy-start.4
  260.0 2.0 copy-start.3
  260.0 2.7 %copy-start.5 = (bf16[128,128]{1,0:T(8,128)(2,1)S(1)}, bf16[128,128]{1,0:T(8,128)(2,1)}, u32[]{:S(2)}) copy-start(bf16[128,128]{1,0:T(8,128)(2,1)} %get-tuple-element.50) | copy-start | bytes 98308
